TPU v7x, 256 devices: a whole 4x4x8 slice. The times are simulated.
256 devices in a mesh: gx: 16 (over x, y), gy: 16 (over z, core).
Axes of the slice: x: 4, y: 4, z: 8, core: 2. Of those that a mesh axis runs over, the one named last changes fastest.
Arguments:
- velocity: bfloat16 [3, 256, 512, 256], P(None, 'gx', 'gy'), may hold values from -4 to 4
- density: bfloat16 [256, 512, 256], P('gx', 'gy'), may hold values from 0 to 1
Outputs:
- projected: float32 [3, 256, 512, 256], P(None, 'gx', 'gy')
- emission: float32 [256, 512, 256], P('gx', 'gy')
All inputs are finite; a program needn't handle non-finite values.
Results may differ from a plain program's by a relative error of at most 0.0003.
Values sent between devices are 32-bit elements; how exact they have to be, the bound alone decides.
No kernel may reach another device: no remote copies, remote signals or barrier semaphores. Data moves between devices by JAX's collectives and lax.ppermute only.
A program may use at most 64 MiB of HBM per device.

v0:
```python
import jax
import jax.numpy as jnp
import numpy as np
from jax import lax
from jax.experimental import pallas as pl
from jax.experimental.pallas import tpu as pltpu
from jax.sharding import PartitionSpec as P

time_step = 0.4
buoyancy = 2.0
extinction = 3.0
highest = lax.Precision.HIGHEST

block_x, block_y, size_z = 16, 32, 256
count_x, count_y = 16, 16
full_x, full_y = 256, 512
chunk_z = 16
send_rows = 72
back_rows = 88


def cosine_array(length):
    modes = np.arange(length, dtype=np.float64)[:, None]
    centres = np.arange(length, dtype=np.float64)[None, :] + 0.5
    factor = np.where(modes == 0, np.sqrt(1.0 / length), np.sqrt(2.0 / length))
    return (factor * np.cos(np.pi * modes * centres / length)).astype(np.float32)


def eigen_array(length):
    modes = np.arange(length, dtype=np.float64)
    return (4.0 * np.sin(np.pi * modes / (2 * length)) ** 2).astype(np.float32)


def swap_groups(tile):
    row = lax.broadcasted_iota(jnp.int32, (8, 128), 0)
    group = lax.broadcasted_iota(jnp.int32, (8, 128), 1) // 16
    for step in (1, 2, 4):
        row_bit = (row & step) != 0
        group_bit = (group & step) != 0
        below = pltpu.roll(pltpu.roll(tile, 8 - step, 0), 16 * step, 1)
        above = pltpu.roll(pltpu.roll(tile, step, 0), 128 - 16 * step, 1)
        tile = jnp.where(
            row_bit == group_bit, tile, jnp.where(group_bit, below, above)
        )
    return tile


def turn_groups(tile):
    row = lax.broadcasted_iota(jnp.int32, (8, 128), 0)
    group = lax.broadcasted_iota(jnp.int32, (8, 128), 1) // 16
    skewed = pltpu.roll(tile, 0, 1, stride=16, stride_axis=0)
    return pltpu.roll(
        jnp.take_along_axis(skewed, (row + group) & 7, axis=0), 0, 1, stride=16, stride_axis=0
    )


turned = [half * 128 + (-group % 8) * 16 + mode for half in range(2) for group in range(8) for mode in range(16)]


def dot(left, right, dims):
    return lax.dot_general(
        left, right, (dims, ((), ())), precision=highest, preferred_element_type=jnp.float32
    )


def weights(speeds, step, half, lane):
    taps = []
    centre = None
    for axis, speed in enumerate(speeds):
        scaled = speed * (step / 6.0)
        ahead = jnp.maximum(scaled, 0.0)
        back = ahead - scaled
        both = ahead + back
        centre = both if centre is None else centre + both
        plus_two, minus_two = back, ahead
        plus_one = 6.0 * back - 2.0 * ahead
        minus_one = 6.0 * ahead - 2.0 * back
        if axis == 2 and half == 0:
            minus_one = jnp.where(lane > 0, minus_one, 0.0)
            minus_two = jnp.where(lane > 1, minus_two, 0.0)
        if axis == 2 and half == 1:
            plus_one = jnp.where(lane < 127, plus_one, 0.0)
            plus_two = jnp.where(lane < 126, plus_two, 0.0)
        taps.append((plus_two, plus_one, minus_one, minus_two))
    return taps, -3.0 * centre


def moved_along_z(pair, half, shift, lane):
    here = pltpu.roll(pair[half], (128 - shift) % 128, 1)
    if (shift > 0) == (half == 1):
        return here
    other = pltpu.roll(pair[1 - half], (128 - shift) % 128, 1)
    return jnp.where(lane < 128 - shift if shift > 0 else lane >= -shift, here, other)


def change(ref, field, x, tile, half, pair, taps, centre, lane):
    total = centre * pair[half]
    for axis, (plus_two, plus_one, minus_one, minus_two) in enumerate(taps):
        if axis == 0:
            parts = [ref[field, x + shift, half, tile] for shift in (2, 1, -1, -2)]
        elif axis == 1:
            parts = [ref[field, x, half, tile + shift] for shift in (2, 1, -1, -2)]
        else:
            parts = [moved_along_z(pair, half, shift, lane) for shift in (2, 1, -1, -2)]
        total = total - plus_two * parts[0]
        total = total + plus_one * parts[1]
        total = total + minus_one * parts[2]
        total = total - minus_two * parts[3]
    return total


tiles = 5


def advect_kernel(
    velocity_hbm, density_hbm, low_x_ref, high_x_ref, low_y_ref, high_y_ref, low_c_ref,
    high_c_ref, table_ref, lifted_ref, smoke_ref, out_ref,
    stage_ref, raw_ref, one_ref, below_ref, div_ref, freq_ref, sum_ref, total_ref,
    velocity_ref, density_ref, arrived,
):
    copies = fetched(velocity_hbm, density_hbm, velocity_ref, density_ref, arrived)
    for copy in copies:
        copy.start()
    place_x, place_y = lax.axis_index("gx"), lax.axis_index("gy")

    def fill_rims(pair, carry):
        for field in range(4):
            for half in range(2):
                low, high = low_y_ref[field, pair, half], high_y_ref[field, pair, half]
                at = 2 * pair + 5
                stage_ref[field, at, half, 4:8, :] = low[0:4]
                stage_ref[field, at + 1, half, 4:8, :] = low[4:8]
                stage_ref[field, at, half, 40:44, :] = high[0:4]
                stage_ref[field, at + 1, half, 40:44, :] = high[4:8]
        return carry

    lax.fori_loop(0, block_x // 2, fill_rims, 0)
    for x in range(block_x):
        for half in range(2):
            stage_ref[1, x + 5, half, 3:4, :] = low_y_ref[4, x // 8, half, x % 8 : x % 8 + 1, :]
    for field in range(4):
        for x in range(4):
            for half in range(2):
                for at, edge_ref, corner_ref in ((1, low_x_ref, low_c_ref), (21, high_x_ref, high_c_ref)):
                    stage_ref[field, x + at, half, 8:40, :] = edge_ref[field * 4 + x, half]
                    corner = corner_ref[field, x, half]
                    stage_ref[field, x + at, half, 4:8, :] = corner[4:8]
                    stage_ref[field, x + at, half, 40:44, :] = corner[0:4]
    for half in range(2):
        stage_ref[0, 0, half, 8:40, :] = low_x_ref[16, half]

    for copy in copies:
        copy.wait()

    def fill(x, carry):
        for field in range(4):
            source = (velocity_ref[field, x] if field < 3 else density_ref[x]).astype(jnp.float32)
            for half in range(2):
                stage_ref[field, x + 5, half, 8:40, :] = source[:, half * 128 : half * 128 + 128]
        return carry

    lax.fori_loop(0, block_x, fill, 0)

    def spread(x, carry):
        for field in range(4):
            for half in range(2):
                for tile in range(-2, tiles + 2):
                    raw_ref[field, x, half, tile + 2] = stage_ref[
                        field, x, half, pl.ds(3 + tile, 8, stride=5), :
                    ]
        return carry

    lax.fori_loop(0, block_x + 9, spread, 0)

    lane = lax.broadcasted_iota(jnp.int32, (8, 128), 1)
    last_row = (lax.broadcasted_iota(jnp.int32, (8, 128), 0) == 7) & (place_y == count_y - 1)
    halves = range(2)

    def closed(value, field, open_x, tile, half):
        if field == 0:
            return jnp.where(open_x, value, 0.0)
        if field == 1 and tile == 1:
            return jnp.where(last_row, 0.0, value)
        if field == 2 and half == 1:
            return jnp.where(lane < 127, value, 0.0)
        return value

    def section_one(x, carry):
        open_x = place_x * block_x + x - 3 != full_x - 1
        for tile in range(tiles):
            pairs = [[raw_ref[field, x + 2, half, tile + 2] for half in halves] for field in range(4)]
            for half in halves:
                taps, centre = weights([pairs[c][half] for c in range(3)], time_step, half, lane)
                for field in range(4):
                    value = pairs[field][half] + change(
                        raw_ref, field, x + 2, tile + 2, half, pairs[field], taps, centre, lane
                    )
                    value = closed(value, field, open_x, tile, half)
                    one_ref[field, x, half, tile + 2] = value
                    if tile < 2:
                        one_ref[field, x, half, tile + 7] = pltpu.roll(value, 7, 0)
                    if tile > 2:
                        one_ref[field, x, half, tile - 3] = pltpu.roll(value, 1, 0)
        return carry

    lax.fori_loop(0, block_x + 5, section_one, 0)

    def section_two(x, tile, fields, open_x):
        pairs = [[one_ref[field, x + 3, half, tile + 2] for half in halves] for field in range(4)]
        values = {field: [] for field in fields}
        for half in halves:
            taps, centre = weights([pairs[c][half] for c in range(3)], 0.5 * time_step, half, lane)
            for field in fields:
                value = 0.5 * (raw_ref[field, x + 5, half, tile + 2] + pairs[field][half]) + change(
                    one_ref, field, x + 3, tile + 2, half, pairs[field], taps, centre, lane
                )
                values[field].append(closed(value, field, open_x, tile, half))
        return values

    for tile in range(tiles):
        for half in halves:
            sum_ref[half, tile] = jnp.zeros((8, 128), jnp.float32)
        for half, value in enumerate(section_two(-1, tile, (0,), True)[0]):
            below_ref[half, tile] = value

    def plane(x, carry):
        open_x = place_x * block_x + x != full_x - 1
        waiting, previous = None, None
        for tile in range(tiles):
            rows = pl.ds(3 + tile, 8, stride=5)
            values = section_two(x, tile, (0, 1, 2, 3), open_x)
            smoke = values[3]
            along_z = [
                values[2][half]
                + (time_step * buoyancy * 0.5)
                * (smoke[half] + moved_along_z(smoke, half, 1, lane))
                for half in halves
            ]
            along_z[1] = jnp.where(lane < 127, along_z[1], 0.0)
            div = []
            for half in halves:
                sum_ref[half, tile] = sum_ref[half, tile] + smoke[half]
                beneath = moved_along_z(along_z, half, -1, lane)
                if half == 0:
                    beneath = jnp.where(lane > 0, beneath, 0.0)
                div.append(
                    values[0][half]
                    - below_ref[half, tile]
                    + (along_z[half] - beneath)
                    + values[1][half]
                )
                below_ref[half, tile] = values[0][half]
                lifted_ref[0, x, half, rows, :] = values[0][half]
                lifted_ref[1, x, half, rows, :] = values[1][half]
                lifted_ref[2, x, half, rows, :] = along_z[half]
                smoke_ref[x, half, rows, :] = smoke[half]
                if tile > 0:
                    div_ref[x, half, rows, :] = div[half] - previous[half]
            if tile == 0:
                waiting = div
            previous = values[1]
        for half in halves:
            div_ref[x, half, pl.ds(3, 8, stride=5), :] = waiting[half] - pltpu.roll(
                previous[half], 1, 0
            )
        return carry

    lax.fori_loop(0, block_x, plane, 0)
    for tile in range(tiles):
        for half in halves:
            total_ref[half, pl.ds(3 + tile, 8, stride=5), :] = sum_ref[half, tile]
    lines = [div_ref[:, half, 8:40, :].reshape(block_x * block_y, 128) for half in halves]
    freq_ref[...] = dot(jnp.concatenate(lines, axis=1), table_ref[...], ((1,), (0,)))

    def pack(x, carry):
        for part in range(4):
            for half in halves:
                tile = freq_ref[
                    pl.ds(pl.multiple_of(x * block_y, 8) + part * 8, 8), half * 128 : half * 128 + 128
                ]
                out_ref[pl.ds(half * 8 * send_rows + part * 16 + x, 8, stride=send_rows), :] = (
                    turn_groups(tile)
                )
        return carry

    lax.fori_loop(0, block_x, pack, 0)
    for part in range(4):
        for half in halves:
            tile = total_ref[half, 8 + part * 8 : 16 + part * 8, :]
            out_ref[pl.ds(half * 8 * send_rows + 64 + part, 8, stride=send_rows), :] = swap_groups(
                tile
            )
    for peer in range(count_x):
        out_ref[peer * send_rows + 68 : peer * send_rows + 72, :] = jnp.zeros((4, 128), jnp.float32)


def edge_kernel(
    velocity_hbm, density_hbm, up_x_ref, down_x_ref, up_y_ref, down_y_ref,
    velocity_ref, density_ref, arrived,
):
    copies = fetched(velocity_hbm, density_hbm, velocity_ref, density_ref, arrived)
    for copy in copies:
        copy.start()
    for copy in copies:
        copy.wait()
    row = lax.broadcasted_iota(jnp.int32, (8, 128), 0)
    low_rows = row < 4

    def rows_of(field, x):
        return (velocity_ref[field, x] if field < 3 else density_ref[x]).astype(jnp.float32)

    for field in range(4):
        for x in range(4):
            top, bottom = rows_of(field, block_x - 4 + x), rows_of(field, x)
            for half in range(2):
                lanes = slice(half * 128, half * 128 + 128)
                up_x_ref[field * 4 + x, half] = top[:, lanes]
                down_x_ref[field * 4 + x, half] = bottom[:, lanes]
        for pair in range(block_x // 2):
            first, second = rows_of(field, 2 * pair), rows_of(field, 2 * pair + 1)
            for half in range(2):
                lanes = slice(half * 128, half * 128 + 128)
                up_y_ref[field, pair, half] = jnp.where(
                    low_rows,
                    pltpu.roll(first[block_y - 8 :, lanes], 4, 0),
                    second[block_y - 8 :, lanes],
                )
                down_y_ref[field, pair, half] = jnp.where(
                    low_rows, first[:8, lanes], pltpu.roll(second[:8, lanes], 4, 0)
                )
    for group in range(2):
        for half in range(2):
            lanes = slice(half * 128, half * 128 + 128)
            tile = jnp.zeros((8, 128), jnp.float32)
            for x in range(8):
                rows = rows_of(1, group * 8 + x)[block_y - 8 :, lanes]
                tile = jnp.where(row == x, pltpu.roll(rows, (x + 5) % 8, 0), tile)
            up_y_ref[4, group, half] = tile
    fifth = rows_of(0, block_x - 5)
    for half in range(2):
        up_x_ref[16, half] = fifth[:, half * 128 : half * 128 + 128]


def corner_kernel(low_y_ref, high_y_ref, up_ref, down_ref):
    row = lax.broadcasted_iota(jnp.int32, (8, 128), 0)
    for field in range(4):
        for x in range(4):
            for half in range(2):
                for at, ref in ((block_x - 4, up_ref), (0, down_ref)):
                    high = high_y_ref[field, (at + x) // 2, half]
                    low = low_y_ref[field, (at + x) // 2, half]
                    if x % 2 == 0:
                        low = pltpu.roll(low, 4, 0)
                    else:
                        high = pltpu.roll(high, 4, 0)
                    ref[field, x, half] = jnp.where(row < 4, high, low)


def power_of(base, exponent, bits):
    result = jnp.ones_like(base)
    for bit in range(bits):
        result = jnp.where((exponent >> bit) & 1 == 1, result * base, result)
        base = base * base
    return result


def roots_of(lam):
    half = 0.5 * lam
    spread = jnp.sqrt(lam + half * half)
    rho = 1.0 / (1.0 + half + spread)
    return rho, spread


def eigen_sum(eigen_ref, eigen_x_ref, place_x):
    row = lax.broadcasted_iota(jnp.int32, (chunk_z, full_x), 0)
    along_z = jnp.zeros((chunk_z, full_x), jnp.float32)
    for at in range(chunk_z):
        along_z = jnp.where(row == at, eigen_ref[place_x * chunk_z + at], along_z)
    return along_z + eigen_x_ref[...]


def squared(value, times):
    for _ in range(times):
        value = value * value
    return value


def forward_kernel(
    eigen_ref, got_ref, eigen_x_ref, table_ref, local_ref, ends_ref, send_ref, before_ref, line_ref
):
    place_x, place_y = lax.axis_index("gx"), lax.axis_index("gy")
    for part in range(4):
        lines = got_ref[:, part * 16 : part * 16 + 16, :].reshape(full_x, 128)
        line_ref[part * 128 : part * 128 + 128, :] = dot(lines, table_ref[...], ((0,), (0,)))
    lam = eigen_sum(eigen_ref, eigen_x_ref, place_x)
    rho, _ = roots_of(lam)
    special = lam == 0.0
    low = jnp.zeros((chunk_z, full_x), jnp.float32)
    for y in range(block_y):
        low = low * rho + line_ref[y * 16 : y * 16 + 16, :]
        local_ref[y * 16 : y * 16 + 16, :] = low
    high = jnp.zeros((chunk_z, full_x), jnp.float32)
    for y in reversed(range(block_y)):
        high = high * rho
        rows = slice(y * 16, y * 16 + 16)
        here = local_ref[rows, :]
        local_ref[rows, :] = jnp.where(special, here, here + high)
        high = high + line_ref[rows, :]
    ends_ref[0] = low
    ends_ref[1] = high
    rho_32 = squared(rho, 5)
    rho_64 = rho_32 * rho_32
    up = low + power_of(rho_64, place_y, 4) * rho_32 * high
    down = high + power_of(rho_64, count_y - 1 - place_y, 4) * rho_32 * low
    for peer in range(count_y):
        send_ref[peer] = jnp.where(peer > place_y, up, down)
    running = jnp.zeros((4, 128), jnp.float32)
    for peer in range(count_x):
        before_ref[peer, 0:4, :] = running
        running = running + got_ref[peer, 64:68, :]


def turned_rows(y):
    at = (y // 8) * 128 + (-y % 8) * 16
    return slice(at, at + 16)


def backward_kernel(
    eigen_ref, local_ref, ends_ref, got_ref, eigen_x_ref, table_ref, next_ref, before_ref, out_ref, line_ref
):
    place_x, place_y = lax.axis_index("gx"), lax.axis_index("gy")
    lam = eigen_sum(eigen_ref, eigen_x_ref, place_x)
    rho, spread = roots_of(lam)
    special = lam == 0.0
    scale = jnp.where(special, 0.0, -0.5 / jnp.where(special, 1.0, spread))
    low, high = ends_ref[0], ends_ref[1]
    rho_32 = squared(rho, 5)
    rho_64 = rho_32 * rho_32
    rho_up = power_of(rho_64, place_y, 4)
    rho_down = power_of(rho_64, count_y - 1 - place_y, 4)
    from_low = jnp.zeros((chunk_z, full_x), jnp.float32)
    from_high = jnp.zeros((chunk_z, full_x), jnp.float32)
    for peer in range(count_y):
        from_low = jnp.where(peer < place_y, from_low * rho_32 + got_ref[peer], from_low)
        other = count_y - 1 - peer
        from_high = jnp.where(other > place_y, from_high * rho_32 + got_ref[other], from_high)
    rho_992 = rho_up * rho_down * rho_32
    wrap = 1.0 / jnp.where(special, 1.0, 1.0 - rho_992 * rho_32)
    enter_low = (from_low + rho_up * (rho_32 * from_high + high) + rho_992 * low) * wrap
    enter_high = (from_high + rho_down * (rho_32 * from_low + low) + rho_992 * high) * wrap
    mean = (0.5 * (from_low + from_high) + low) * (1.0 / full_y)
    flux_in = 0.5 * from_low - mean * (place_y * block_y).astype(jnp.float32)
    for y in reversed(range(block_y)):
        enter_high_next = enter_high
        rows = slice((y + 1) * 16, (y + 1) * 16 + 16)
        if y + 1 == block_y:
            line_ref[turned_rows(y + 1), :] = rho * low + enter_high_next
        else:
            line_ref[turned_rows(y + 1), :] = local_ref[rows, :] + jnp.where(
                special, 0.0, enter_high_next
            )
        enter_high = enter_high * rho
    line_ref[0:16, :] = local_ref[0:16, :] + jnp.where(special, 0.0, enter_high)
    level = jnp.zeros((chunk_z, full_x), jnp.float32)
    for y in range(block_y + 1):
        rows = turned_rows(y)
        enter_low = enter_low * rho
        here = line_ref[rows, :]
        line_ref[rows, :] = jnp.where(special, level, scale * (here + enter_low))
        level = level + (here + flux_in - mean * (y + 1.0))
    line_ref[(block_y + 1) * 16 :, :] = jnp.zeros((112, full_x), jnp.float32)
    for part in range(5):
        lines = line_ref[part * 128 : part * 128 + 128, :]
        out_ref[:, part * 16 : part * 16 + 16, :] = dot(table_ref[...], lines, ((1,), (1,))).reshape(
            count_x, block_x, 128
        )
        if part < 4:
            out_ref[:, 80 + part : 81 + part, :] = dot(next_ref[...], lines, ((1,), (1,))).reshape(
                count_x, 1, 128
            )
    out_ref[:, 84:88, :] = before_ref[:, 0:4, :]


def final_kernel(
    got_ref, lifted_ref, smoke_ref, table_ref, out_hbm, glow_hbm,
    freq_ref, press_ref, out_ref, glow_ref, out_sent, glow_sent,
):
    place_x, place_y = lax.axis_index("gx"), lax.axis_index("gy")

    def tile_at(row, half, change=turn_groups):
        return change(got_ref[pl.ds(half * 8 * back_rows + row, 8, stride=back_rows), :])

    entered = jnp.concatenate(
        [
            jnp.concatenate([tile_at(84 + part, half, swap_groups) for half in range(2)], axis=1)
            for part in range(4)
        ],
        axis=0,
    )
    attenuation = extinction / full_x

    def whole(ref, *at):
        return jnp.concatenate([ref[(*at, half, slice(8, 40))] for half in range(2)], axis=1)

    def out_copy(x):
        return pltpu.make_async_copy(out_ref.at[x], out_hbm.at[:, x], out_sent.at[x])

    def glow_copy(x):
        return pltpu.make_async_copy(glow_ref.at[x], glow_hbm.at[x], glow_sent.at[x])

    def whole(ref, *at):
        return jnp.concatenate([ref[(*at, half, slice(8, 40))] for half in range(2)], axis=1)

    def shine(x, running):
        smoke = whole(smoke_ref, x)
        depth = attenuation * smoke
        series = 1.0 - depth * (1.0 / 7.0)
        for order in (6.0, 5.0, 4.0, 3.0, 2.0):
            series = 1.0 - depth * (1.0 / order) * series
        lost = jnp.where(jnp.abs(depth) < 0.25, depth * series, 1.0 - jnp.exp(-depth))
        glow_ref[x] = jnp.exp(-attenuation * running) * lost * (1.0 / attenuation)
        glow_copy(x).start()
        return running + smoke

    lax.fori_loop(0, block_x, shine, entered)

    def one(x, carry):
        for part in range(5):
            for half in range(2):
                freq_ref[x, part * 8 : part * 8 + 8, half * 128 : half * 128 + 128] = tile_at(
                    part * 16 + x, half
                )
        return carry

    lax.fori_loop(0, block_x, one, 0)
    for part in range(4):
        for half in range(2):
            freq_ref[block_x, part * 8 : part * 8 + 8, half * 128 : half * 128 + 128] = tile_at(
                80 + part, half
            )
    freq_ref[block_x, 32:40, :] = jnp.zeros((8, size_z), jnp.float32)
    press_ref[...] = dot(
        freq_ref[...].reshape((block_x + 1) * 40, size_z), table_ref[...], ((1,), (0,))
    ).reshape(block_x + 1, 40, size_z)
    along_y = lax.broadcasted_iota(jnp.int32, (block_y, size_z), 0) + place_y * block_y
    along_z = lax.broadcasted_iota(jnp.int32, (block_y, size_z), 1)
    open_y = along_y < full_y - 1
    open_z = along_z < size_z - 1

    def finish(x, carry):
        here = press_ref[x, 0:block_y, :]
        open_x = place_x * block_x + x < full_x - 1
        out_ref[x, 0] = jnp.where(
            open_x, whole(lifted_ref, 0, x) - (press_ref[x + 1, 0:block_y, :] - here), 0.0
        )
        out_ref[x, 1] = jnp.where(
            open_y, whole(lifted_ref, 1, x) - (press_ref[x, 1 : block_y + 1, :] - here), 0.0
        )
        out_ref[x, 2] = jnp.where(
            open_z, whole(lifted_ref, 2, x) - (pltpu.roll(here, size_z - 1, 1) - here), 0.0
        )
        out_copy(x).start()
        return carry

    lax.fori_loop(0, block_x, finish, 0)

    def drain(x, carry):
        glow_copy(x).wait()
        out_copy(x).wait()
        return carry

    lax.fori_loop(0, block_x, drain, 0)


def shaped(*dims):
    return jax.ShapeDtypeStruct(dims, jnp.float32)


def call(kernel, outs, scratch, grant, spaces={}, outside=False):
    vmem = pl.BlockSpec(memory_space=pltpu.VMEM)

    def run(*args):
        specs = [
            pl.BlockSpec(memory_space=spaces[at]) if at in spaces else vmem
            for at in range(len(args))
        ]
        place = pl.BlockSpec(memory_space=pltpu.HBM) if outside else vmem
        return pl.pallas_call(
            kernel,
            out_shape=outs,
            in_specs=specs,
            out_specs=jax.tree.map(lambda _: place, outs),
            scratch_shapes=[
                pltpu.VMEM(entry, jnp.float32) if isinstance(entry, tuple) else entry
                for entry in scratch
            ],
            compiler_params=pltpu.CompilerParams(vmem_limit_bytes=grant << 20),
            cost_estimate=pl.CostEstimate(
                flops=10**9, bytes_accessed=1024, transcendentals=0
            ),
        )(*args)

    return run


inputs_here = [
    pltpu.VMEM((3, block_x, block_y, size_z), jnp.bfloat16),
    pltpu.VMEM((block_x, block_y, size_z), jnp.bfloat16),
    pltpu.SemaphoreType.DMA((2,)),
]


def fetched(velocity_hbm, density_hbm, velocity_ref, density_ref, arrived):
    return [
        pltpu.make_async_copy(velocity_hbm, velocity_ref, arrived.at[0]),
        pltpu.make_async_copy(density_hbm, density_ref, arrived.at[1]),
    ]


def step(velocity, density, rims):
    table_z = cosine_array(size_z)
    table_x = cosine_array(full_x)
    next_x = np.concatenate(
        [table_x.T[block_x::block_x], np.zeros((1, full_x), np.float32)], axis=0
    )
    eigen_z = jnp.asarray(eigen_array(size_z))
    eigen_x = jnp.asarray(np.broadcast_to(eigen_array(full_x)[None, :], (chunk_z, full_x)))
    lifted, smoke, packed = call(
        advect_kernel,
        (
            shaped(3, block_x, 2, 48, 128),
            shaped(block_x, 2, 48, 128),
            shaped(count_x * send_rows, 128),
        ),
        [
            (4, block_x + 9, 2, 48, 128),
            (4, block_x + 9, 2, 9, 8, 128),
            (4, block_x + 5, 2, 9, 8, 128),
            (2, tiles, 8, 128),
            (block_x, 2, 48, 128),
            (block_x * block_y, size_z),
            (2, tiles, 8, 128),
            (2, 48, 128),
            *inputs_here,
        ],
        25,
        {0: pltpu.HBM, 1: pltpu.HBM},
    )(velocity, density, *rims, jnp.asarray(np.ascontiguousarray(table_z.T[:, turned])))
    got = lax.all_to_all(
        packed.reshape(count_x, send_rows, 128), "gx", split_axis=0, concat_axis=0, tiled=True
    )
    table_xt = jnp.asarray(np.ascontiguousarray(table_x.T))
    local, ends, moments, before = call(
        forward_kernel,
        (
            shaped(block_y * chunk_z, full_x),
            shaped(2, chunk_z, full_x),
            shaped(count_y, chunk_z, full_x),
            shaped(count_x, 8, 128),
        ),
        [(block_y * chunk_z, full_x)],
        4,
        {0: pltpu.SMEM},
    )(eigen_z, got, eigen_x, table_xt)
    moments = lax.all_to_all(moments, "gy", split_axis=0, concat_axis=0, tiled=True)
    back = call(
        backward_kernel,
        shaped(count_x, back_rows, 128),
        [(5 * 128, full_x)],
        4,
        {0: pltpu.SMEM},
    )(eigen_z, local, ends, moments, eigen_x, table_xt, jnp.asarray(next_x), before)
    back = lax.all_to_all(back, "gx", split_axis=0, concat_axis=0, tiled=True)
    return call(
        final_kernel,
        (shaped(3, block_x, block_y, size_z), shaped(block_x, block_y, size_z)),
        [
            (block_x + 1, 40, size_z),
            (block_x + 1, 40, size_z),
            (block_x, 3, block_y, size_z),
            (block_x, block_y, size_z),
            pltpu.SemaphoreType.DMA((block_x,)),
            pltpu.SemaphoreType.DMA((block_x,)),
        ],
        8,
        outside=True,
    )(back.reshape(count_x * back_rows, 128), lifted, smoke, jnp.asarray(table_z))


def moved(part, axis, upward):
    pairs = [(i, i + 1) if upward else (i + 1, i) for i in range(15)]
    return lax.ppermute(part, axis, pairs)


def per_device(velocity, density):
    planes, rows = (2, block_y, 128), (block_x // 2, 2, 8, 128)
    up_x, down_x, up_y, down_y = call(
        edge_kernel,
        (shaped(17, *planes), shaped(16, *planes), shaped(5, *rows), shaped(4, *rows)),
        inputs_here,
        4,
        {0: pltpu.HBM, 1: pltpu.HBM},
    )(velocity, density)
    low_x = moved(up_x, "gx", True)
    high_x = moved(down_x, "gx", False)
    low_y = moved(up_y, "gy", True)
    high_y = moved(down_y, "gy", False)
    corner = shaped(4, 4, 2, 8, 128)
    up_c, down_c = call(corner_kernel, (corner, corner), [], 2)(low_y, high_y)
    low_c = moved(up_c, "gx", True)
    high_c = moved(down_c, "gx", False)
    return step(velocity, density, (low_x, high_x, low_y, high_y, low_c, high_c))


def solution(mesh):
    in_specs = (P(None, "gx", "gy", None), P("gx", "gy", None))
    out_specs = (P(None, "gx", "gy", None), P("gx", "gy", None))
    return jax.shard_map(
        per_device, mesh=mesh, in_specs=in_specs, out_specs=out_specs, check_vma=False
    )
```

profile of v0, /device:TPU:1, one launch (start us, length us, event | category | flops | bytes accessed | tf_op | source)
XLA Modules:
  0.0 115.1 jit_solution(8620277647027702624)
XLA Ops:
  0.6 0.0 copy-start.2
  0.6 1.1 copy-done.2
  1.8 0.0 copy-start.4
  1.8 0.9 copy-done.4
  2.7 0.2 shard_map.95
  2.9 0.0 copy-start.3
  2.9 0.0 copy-start.5
  3.0 0.0 copy-start.7
  3.0 4.2 %collective-permute-start = (f32[17,2,32,128]{3,2,1,0:T(8,128)S(1)}, f32[17,2,32,128]{3,2,1,0:T(8,128)S(1)}, u32[]{:S(2)}, u32[]{:S(2)}) collective-permute-start(f32[17,2,32,128]{3,2,1,0:T(8,128)S(1)} %get-tuple-element.15), channel_id=1, source_target_pairs={{0,16},{16,32},{32,48},{48,64},{64,80},{80,96},{96,112},{112,128},... | collective-permute-start | bytes 1671176 | tf_op jit(solution)/shard_map/ppermute | solution.py:692
  7.2 4.4 %collective-permute-start.2 = (f32[5,8,2,8,128]{4,3,2,1,0:T(8,128)S(1)}, f32[5,8,2,8,128]{4,3,2,1,0:T(8,128)S(1)}, u32[]{:S(2)}, u32[]{:S(2)}) collective-permute-start(f32[5,8,2,8,128]{4,3,2,1,0:T(8,128)S(1)} %get-tuple-element.17), channel_id=1, source_target_pairs={{0,1},{1,2},{2,3},{3,4},{4,5},{5,6},{6,7},{7,8},{8,9},{9,10},{10,1... | collective-permute-start | bytes 983048 | tf_op jit(solution)/shard_map/ppermute | solution.py:692
  11.6 1.3 %collective-permute-start.1 = (f32[16,2,32,128]{3,2,1,0:T(8,128)S(1)}, f32[16,2,32,128]{3,2,1,0:T(8,128)S(1)}, u32[]{:S(2)}, u32[]{:S(2)}) collective-permute-start(f32[16,2,32,128]{3,2,1,0:T(8,128)S(1)} %get-tuple-element.16), channel_id=1, source_target_pairs={{16,0},{32,16},{48,32},{64,48},{80,64},{96,80},{112,96},{128,112},... | collective-permute-start | bytes 1572872 | tf_op jit(solution)/shard_map/ppermute | solution.py:692
  12.9 1.9 %collective-permute-start.3 = (f32[4,8,2,8,128]{4,3,2,1,0:T(8,128)S(1)}, f32[4,8,2,8,128]{4,3,2,1,0:T(8,128)S(1)}, u32[]{:S(2)}, u32[]{:S(2)}) collective-permute-start(f32[4,8,2,8,128]{4,3,2,1,0:T(8,128)S(1)} %get-tuple-element.18), channel_id=1, source_target_pairs={{1,0},{2,1},{3,2},{4,3},{5,4},{6,5},{7,6},{8,7},{9,8},{10,9},{11,1... | collective-permute-start | bytes 786440 | tf_op jit(solution)/shard_map/ppermute | solution.py:692
  14.8 6.1 %collective-permute-done.3.high_y_ref = f32[4,8,2,8,128]{4,3,2,1,0:T(8,128)S(1)} collective-permute-done((f32[4,8,2,8,128]{4,3,2,1,0:T(8,128)S(1)}, f32[4,8,2,8,128]{4,3,2,1,0:T(8,128)S(1)}, u32[]{:S(2)}, u32[]{:S(2)}) %collective-permute-start.3) | collective-permute-done | bytes 262176 | tf_op jit(solution)/shard_map/ppermute | solution.py:692
  20.8 0.0 collective-permute-done.2.low_y_ref
  20.9 4.0 %collective-permute-start.4 = (f32[4,4,2,8,128]{4,3,2,1,0:T(8,128)S(1)}, f32[4,4,2,8,128]{4,3,2,1,0:T(8,128)S(1)}, u32[]{:S(2)}, u32[]{:S(2)}) collective-permute-start(f32[4,4,2,8,128]{4,3,2,1,0:T(8,128)S(1)} %get-tuple-element.19), channel_id=1, source_target_pairs={{0,16},{16,32},{32,48},{48,64},{64,80},{80,96},{96,112},{112,128},... | collective-permute-start | bytes 393224 | tf_op jit(solution)/shard_map/ppermute | solution.py:692
  24.9 0.0 copy-start.1
  24.9 0.0 copy-start.6
  24.9 1.4 %collective-permute-start.5 = (f32[4,4,2,8,128]{4,3,2,1,0:T(8,128)S(1)}, f32[4,4,2,8,128]{4,3,2,1,0:T(8,128)S(1)}, u32[]{:S(2)}, u32[]{:S(2)}) collective-permute-start(f32[4,4,2,8,128]{4,3,2,1,0:T(8,128)S(1)} %get-tuple-element.20), channel_id=1, source_target_pairs={{16,0},{32,16},{48,32},{64,48},{80,64},{96,80},{112,96},{128,112},... | collective-permute-start | bytes 393224 | tf_op jit(solution)/shard_map/ppermute | solution.py:692
  26.3 0.5 collective-permute-done.4.low_c_ref
  26.8 3.9 %collective-permute-done.5.high_c_ref = f32[4,4,2,8,128]{4,3,2,1,0:T(8,128)S(1)} collective-permute-done((f32[4,4,2,8,128]{4,3,2,1,0:T(8,128)S(1)}, f32[4,4,2,8,128]{4,3,2,1,0:T(8,128)S(1)}, u32[]{:S(2)}, u32[]{:S(2)}) %collective-permute-start.5) | collective-permute-done | bytes 131104 | tf_op jit(solution)/shard_map/ppermute | solution.py:692
  30.7 0.0 collective-permute-done.1.high_x_ref
  30.7 0.0 collective-permute-done.low_x_ref
  30.7 0.0 copy-done.3
  30.8 0.0 copy-done.5
  30.8 0.0 copy-done.7
  30.8 15.3 %shard_map.97 = (f32[3,16,2,48,128]{4,3,2,1,0:T(8,128)S(1)}, f32[16,2,48,128]{3,2,1,0:T(8,128)S(1)}, f32[1152,128]{1,0:T(8,128)S(1)}) custom-call(bf16[3,16,32,256]{3,2,1,0:T(8,128)(2,1)S(1)} %copy-done.3, bf16[16,32,256]{2,1,0:T(8,128)(2,1)S(1)} %copy-done.5, f32[17,2,32,128]{3,2,1,0:T(8,128)S(1)} %collective-permute-done.low_x_ref, ...), custom_call_target="tpu_custom_call" | custom-call | flops 1000000000 | bytes 1024 | tf_op jit(solution)/shard_map/pallas_call | solution.py:588
  46.1 20.0 %all_to_all.15.got_ref = f32[16,72,128]{2,1,0:T(8,128)S(1)} all-to-all(f32[16,72,128]{2,1,0:T(8,128)S(1)} %bitcast.3), channel_id=1, replica_groups=mesh['gx'=16,'gy'=16] {'gx'}, dimensions={0} | all-to-all | bytes 1179648 | tf_op jit(solution)/shard_map/all_to_all | solution.py:649
  66.0 0.0 copy-done.1
  66.0 0.0 copy-start.8
  66.0 0.0 copy-done.6
  66.0 1.4 %shard_map.98 = (f32[512,256]{1,0:T(8,128)S(1)}, f32[2,16,256]{2,1,0:T(8,128)S(1)}, f32[16,16,256]{2,1,0:T(8,128)S(1)}, f32[16,8,128]{2,1,0:T(8,128)S(1)}) custom-call(f32[256]{0:T(256)S(1)} %copy-done.1, f32[16,72,128]{2,1,0:T(8,128)S(1)} %all_to_all.15.got_ref, f32[16,256]{1,0:T(8,128)S(1)} %jit_solution_.3.eigen_x_ref, f32[256,256]{1,0:T(8,128)S(1)} %copy-done.6), custom_call_target="tpu_custom_call" | custom-call | flops 1000000000 | bytes 1024 | tf_op jit(solution)/shard_map/pallas_call | solution.py:588
  67.5 22.8 %all_to_all.16.got_ref = f32[16,16,256]{2,1,0:T(8,128)S(1)} all-to-all(f32[16,16,256]{2,1,0:T(8,128)S(1)} %get-tuple-element.24), channel_id=1, replica_groups=mesh['gx'=16,'gy'=16] {'gy'}, dimensions={0} | all-to-all | bytes 524288 | tf_op jit(solution)/shard_map/all_to_all | solution.py:665
  90.3 0.0 copy-done.8
  90.3 0.0 copy-start
  90.3 2.4 %shard_map.99 = f32[16,88,128]{2,1,0:T(8,128)S(1)} custom-call(f32[256]{0:T(256)S(1)} %copy-done.1, f32[512,256]{1,0:T(8,128)S(1)} %get-tuple-element.22.local_ref, f32[2,16,256]{2,1,0:T(8,128)S(1)} %get-tuple-element.23.ends_ref, f32[16,16,256]{2,1,0:T(8,128)S(1)} %all_to_all.16.got_ref, f32[16,256]{1,0:T(8,128)S(1)} %jit_solution_.3.eigen_x_ref, ...), custom_call_target="tpu_custom_call" | custom-call | flops 1000000000 | bytes 1024 | tf_op jit(solution)/shard_map/pallas_call | solution.py:588
  92.7 16.2 %all_to_all.17 = f32[16,88,128]{2,1,0:T(8,128)S(1)} all-to-all(f32[16,88,128]{2,1,0:T(8,128)S(1)} %shard_map.99), channel_id=1, replica_groups=mesh['gx'=16,'gy'=16] {'gx'}, dimensions={0} | all-to-all | bytes 1441792 | tf_op jit(solution)/shard_map/all_to_all | solution.py:673
  108.9 0.0 copy-done
  108.9 6.3 %shard_map.100 = (f32[3,16,32,256]{3,2,1,0:T(8,128)}, f32[16,32,256]{2,1,0:T(8,128)}) custom-call(f32[1408,128]{1,0:T(8,128)S(1)} %bitcast.2, f32[3,16,2,48,128]{4,3,2,1,0:T(8,128)S(1)} %get-tuple-element.26.lifted_ref, f32[16,2,48,128]{3,2,1,0:T(8,128)S(1)} %get-tuple-element.27.smoke_ref, f32[256,256]{1,0:T(8,128)S(1)} %copy-done), custom_call_target="tpu_custom_call" | custom-call | flops 1000000000 | bytes 1024 | tf_op jit(solution)/shard_map/pallas_call | solution.py:588
  (2 shorter events, 0.0 us)
Async XLA Ops:
  0.6 1.1 copy-start.2
  1.8 0.9 copy-start.4
  2.9 27.8 %copy-start.3 = (bf16[3,16,32,256]{3,2,1,0:T(8,128)(2,1)S(1)}, bf16[3,16,32,256]{3,2,1,0:T(8,128)(2,1)}, u32[]{:S(2)}) copy-start(bf16[3,16,32,256]{3,2,1,0:T(8,128)(2,1)} %velocity_hbm.3) | copy-start | bytes 2359300
  2.9 27.8 %copy-start.5 = (bf16[16,32,256]{2,1,0:T(8,128)(2,1)S(1)}, bf16[16,32,256]{2,1,0:T(8,128)(2,1)}, u32[]{:S(2)}) copy-start(bf16[16,32,256]{2,1,0:T(8,128)(2,1)} %density_hbm.3) | copy-start | bytes 786436
  3.0 27.8 %copy-start.7 = (f32[256,256]{1,0:T(8,128)S(1)}, f32[256,256]{1,0:T(8,128)}, u32[]{:S(2)}) copy-start(f32[256,256]{1,0:T(8,128)} %constant.12.clone.table_ref) | copy-start | bytes 786436
  3.0 27.8 %collective-permute-start = (f32[17,2,32,128]{3,2,1,0:T(8,128)S(1)}, f32[17,2,32,128]{3,2,1,0:T(8,128)S(1)}, u32[]{:S(2)}, u32[]{:S(2)}) collective-permute-start(f32[17,2,32,128]{3,2,1,0:T(8,128)S(1)} %get-tuple-element.15), channel_id=1, source_target_pairs={{0,16},{16,32},{32,48},{48,64},{64,80},{80,96},{96,112},{112,128},... | collective-permute-start | bytes 1671176 | tf_op jit(solution)/shard_map/ppermute | solution.py:692
  7.2 13.7 %collective-permute-start.2 = (f32[5,8,2,8,128]{4,3,2,1,0:T(8,128)S(1)}, f32[5,8,2,8,128]{4,3,2,1,0:T(8,128)S(1)}, u32[]{:S(2)}, u32[]{:S(2)}) collective-permute-start(f32[5,8,2,8,128]{4,3,2,1,0:T(8,128)S(1)} %get-tuple-element.17), channel_id=1, source_target_pairs={{0,1},{1,2},{2,3},{3,4},{4,5},{5,6},{6,7},{7,8},{8,9},{9,10},{10,1... | collective-permute-start | bytes 983048 | tf_op jit(solution)/shard_map/ppermute | solution.py:692
  11.6 19.2 %collective-permute-start.1 = (f32[16,2,32,128]{3,2,1,0:T(8,128)S(1)}, f32[16,2,32,128]{3,2,1,0:T(8,128)S(1)}, u32[]{:S(2)}, u32[]{:S(2)}) collective-permute-start(f32[16,2,32,128]{3,2,1,0:T(8,128)S(1)} %get-tuple-element.16), channel_id=1, source_target_pairs={{16,0},{32,16},{48,32},{64,48},{80,64},{96,80},{112,96},{128,112},... | collective-permute-start | bytes 1572872 | tf_op jit(solution)/shard_map/ppermute | solution.py:692
  12.9 8.0 %collective-permute-start.3 = (f32[4,8,2,8,128]{4,3,2,1,0:T(8,128)S(1)}, f32[4,8,2,8,128]{4,3,2,1,0:T(8,128)S(1)}, u32[]{:S(2)}, u32[]{:S(2)}) collective-permute-start(f32[4,8,2,8,128]{4,3,2,1,0:T(8,128)S(1)} %get-tuple-element.18), channel_id=1, source_target_pairs={{1,0},{2,1},{3,2},{4,3},{5,4},{6,5},{7,6},{8,7},{9,8},{10,9},{11,1... | collective-permute-start | bytes 786440 | tf_op jit(solution)/shard_map/ppermute | solution.py:692
  20.9 5.9 %collective-permute-start.4 = (f32[4,4,2,8,128]{4,3,2,1,0:T(8,128)S(1)}, f32[4,4,2,8,128]{4,3,2,1,0:T(8,128)S(1)}, u32[]{:S(2)}, u32[]{:S(2)}) collective-permute-start(f32[4,4,2,8,128]{4,3,2,1,0:T(8,128)S(1)} %get-tuple-element.19), channel_id=1, source_target_pairs={{0,16},{16,32},{32,48},{48,64},{64,80},{80,96},{96,112},{112,128},... | collective-permute-start | bytes 393224 | tf_op jit(solution)/shard_map/ppermute | solution.py:692
  24.9 41.2 %copy-start.1 = (f32[256]{0:T(256)S(1)}, f32[256]{0:T(256)}, u32[]{:S(2)}) copy-start(f32[256]{0:T(256)} %constant.10.clone.eigen_ref) | copy-start | bytes 3076
  24.9 41.2 %copy-start.6 = (f32[256,256]{1,0:T(8,128)S(1)}, f32[256,256]{1,0:T(8,128)}, u32[]{:S(2)}) copy-start(f32[256,256]{1,0:T(8,128)} %constant.13.clone.table_ref) | copy-start | bytes 786436
  24.9 5.8 %collective-permute-start.5 = (f32[4,4,2,8,128]{4,3,2,1,0:T(8,128)S(1)}, f32[4,4,2,8,128]{4,3,2,1,0:T(8,128)S(1)}, u32[]{:S(2)}, u32[]{:S(2)}) collective-permute-start(f32[4,4,2,8,128]{4,3,2,1,0:T(8,128)S(1)} %get-tuple-element.20), channel_id=1, source_target_pairs={{16,0},{32,16},{48,32},{64,48},{80,64},{96,80},{112,96},{128,112},... | collective-permute-start | bytes 393224 | tf_op jit(solution)/shard_map/ppermute | solution.py:692
  66.0 24.3 %copy-start.8 = (f32[16,256]{1,0:T(8,128)S(1)}, f32[16,256]{1,0:T(8,128)}, u32[]{:S(2)}) copy-start(f32[16,256]{1,0:T(8,128)} %constant.14.clone.next_ref) | copy-start | bytes 49156
  90.3 18.6 %copy-start = (f32[256,256]{1,0:T(8,128)S(1)}, f32[256,256]{1,0:T(8,128)}, u32[]{:S(2)}) copy-start(f32[256,256]{1,0:T(8,128)} %constant.15.clone.table_ref) | copy-start | bytes 786436
where the time goes:
time: 116 us; the launch traced here: 115 us
  blocking collectives  59 us (51%)
  Pallas kernels  25.6 us (22%)
  starting transfers between devices  17.2 us (15%)
  waiting for transfers between devices  10.5 us (9%)
  local copies, waits for them, and re-layouts  2.12 us (2%)
    pallas_call x6, Pallas kernels, run(): pl.pallas_call(kernel, out_shape=outs, in_specs=specs, out_specs=jax.tree...  25.6 us
    all_to_all x1, blocking collectives, step(): lax.all_to_all(moments, 'gy', split_axis=0, concat_axis=0, tiled=True)  22.8 us
    all_to_all x1, blocking collectives, step(): lax.all_to_all(packed.reshape(count_x, send_rows, 128), 'gx', split_axis=...  20 us
    ppermute x6, starting transfers between devices, moved(): return lax.ppermute(part, axis, pairs)  17.2 us
    all_to_all x1, blocking collectives, step(): back = lax.all_to_all(back, 'gx', split_axis=0, concat_axis=0, tiled=True)  16.2 us
    ppermute x6, waiting for transfers between devices, moved(): return lax.ppermute(part, axis, pairs)  10.5 us
  transfers between devices with their start and end apart: 6, of which 3 were waited for; matrix products, arithmetic and copies ran while one was open for 0% of the time, Pallas kernels for 0%

commit v1 on v0

--- a/solution.py
+++ b/solution.py
@@ -1,3 +1,5 @@
+import functools
+
 import jax
 import jax.numpy as jnp
 import numpy as np
@@ -34,15 +36,11 @@
 def swap_groups(tile):
     row = lax.broadcasted_iota(jnp.int32, (8, 128), 0)
     group = lax.broadcasted_iota(jnp.int32, (8, 128), 1) // 16
-    for step in (1, 2, 4):
-        row_bit = (row & step) != 0
-        group_bit = (group & step) != 0
-        below = pltpu.roll(pltpu.roll(tile, 8 - step, 0), 16 * step, 1)
-        above = pltpu.roll(pltpu.roll(tile, step, 0), 128 - 16 * step, 1)
-        tile = jnp.where(
-            row_bit == group_bit, tile, jnp.where(group_bit, below, above)
-        )
-    return tile
+    skewed = pltpu.roll(tile, 0, 1, stride=16, stride_axis=0)
+    upturned = pltpu.roll(
+        jnp.take_along_axis(skewed, (row + group + 1) & 7, axis=0), 16, 1, stride=16, stride_axis=0
+    )
+    return jnp.take_along_axis(upturned, 7 - row, axis=0)
 
 
 def turn_groups(tile):
@@ -110,71 +108,17 @@
 
 
 tiles = 5
-
-
-def advect_kernel(
-    velocity_hbm, density_hbm, low_x_ref, high_x_ref, low_y_ref, high_y_ref, low_c_ref,
-    high_c_ref, table_ref, lifted_ref, smoke_ref, out_ref,
-    stage_ref, raw_ref, one_ref, below_ref, div_ref, freq_ref, sum_ref, total_ref,
-    velocity_ref, density_ref, arrived,
-):
-    copies = fetched(velocity_hbm, density_hbm, velocity_ref, density_ref, arrived)
-    for copy in copies:
-        copy.start()
+halves = range(2)
+
+
+def rows_of_tile(tile):
+    return pl.ds(3 + tile, 8, stride=5)
+
+
+def stencil(raw_ref, raw_first, one_ref, one_first):
     place_x, place_y = lax.axis_index("gx"), lax.axis_index("gy")
-
-    def fill_rims(pair, carry):
-        for field in range(4):
-            for half in range(2):
-                low, high = low_y_ref[field, pair, half], high_y_ref[field, pair, half]
-                at = 2 * pair + 5
-                stage_ref[field, at, half, 4:8, :] = low[0:4]
-                stage_ref[field, at + 1, half, 4:8, :] = low[4:8]
-                stage_ref[field, at, half, 40:44, :] = high[0:4]
-                stage_ref[field, at + 1, half, 40:44, :] = high[4:8]
-        return carry
-
-    lax.fori_loop(0, block_x // 2, fill_rims, 0)
-    for x in range(block_x):
-        for half in range(2):
-            stage_ref[1, x + 5, half, 3:4, :] = low_y_ref[4, x // 8, half, x % 8 : x % 8 + 1, :]
-    for field in range(4):
-        for x in range(4):
-            for half in range(2):
-                for at, edge_ref, corner_ref in ((1, low_x_ref, low_c_ref), (21, high_x_ref, high_c_ref)):
-                    stage_ref[field, x + at, half, 8:40, :] = edge_ref[field * 4 + x, half]
-                    corner = corner_ref[field, x, half]
-                    stage_ref[field, x + at, half, 4:8, :] = corner[4:8]
-                    stage_ref[field, x + at, half, 40:44, :] = corner[0:4]
-    for half in range(2):
-        stage_ref[0, 0, half, 8:40, :] = low_x_ref[16, half]
-
-    for copy in copies:
-        copy.wait()
-
-    def fill(x, carry):
-        for field in range(4):
-            source = (velocity_ref[field, x] if field < 3 else density_ref[x]).astype(jnp.float32)
-            for half in range(2):
-                stage_ref[field, x + 5, half, 8:40, :] = source[:, half * 128 : half * 128 + 128]
-        return carry
-
-    lax.fori_loop(0, block_x, fill, 0)
-
-    def spread(x, carry):
-        for field in range(4):
-            for half in range(2):
-                for tile in range(-2, tiles + 2):
-                    raw_ref[field, x, half, tile + 2] = stage_ref[
-                        field, x, half, pl.ds(3 + tile, 8, stride=5), :
-                    ]
-        return carry
-
-    lax.fori_loop(0, block_x + 9, spread, 0)
-
     lane = lax.broadcasted_iota(jnp.int32, (8, 128), 1)
     last_row = (lax.broadcasted_iota(jnp.int32, (8, 128), 0) == 7) & (place_y == count_y - 1)
-    halves = range(2)
 
     def closed(value, field, open_x, tile, half):
         if field == 0:
@@ -185,105 +129,244 @@
             return jnp.where(lane < 127, value, 0.0)
         return value
 
-    def section_one(x, carry):
-        open_x = place_x * block_x + x - 3 != full_x - 1
+    def is_open(x):
+        return place_x * block_x + x != full_x - 1
+
+    def section_one(x, fields=(0, 1, 2, 3)):
+        at = x - raw_first
         for tile in range(tiles):
-            pairs = [[raw_ref[field, x + 2, half, tile + 2] for half in halves] for field in range(4)]
+            pairs = [[raw_ref[field, at, half, tile + 2] for half in halves] for field in range(4)]
             for half in halves:
                 taps, centre = weights([pairs[c][half] for c in range(3)], time_step, half, lane)
-                for field in range(4):
+                for field in fields:
                     value = pairs[field][half] + change(
-                        raw_ref, field, x + 2, tile + 2, half, pairs[field], taps, centre, lane
+                        raw_ref, field, at, tile + 2, half, pairs[field], taps, centre, lane
                     )
-                    value = closed(value, field, open_x, tile, half)
-                    one_ref[field, x, half, tile + 2] = value
+                    value = closed(value, field, is_open(x), tile, half)
+                    one_ref[field, x - one_first, half, tile + 2] = value
                     if tile < 2:
-                        one_ref[field, x, half, tile + 7] = pltpu.roll(value, 7, 0)
+                        one_ref[field, x - one_first, half, tile + 7] = pltpu.roll(value, 7, 0)
                     if tile > 2:
-                        one_ref[field, x, half, tile - 3] = pltpu.roll(value, 1, 0)
-        return carry
-
-    lax.fori_loop(0, block_x + 5, section_one, 0)
-
-    def section_two(x, tile, fields, open_x):
-        pairs = [[one_ref[field, x + 3, half, tile + 2] for half in halves] for field in range(4)]
+                        one_ref[field, x - one_first, half, tile - 3] = pltpu.roll(value, 1, 0)
+
+    def section_two(x, tile, fields):
+        at = x - one_first
+        pairs = [[one_ref[field, at, half, tile + 2] for half in halves] for field in range(4)]
         values = {field: [] for field in fields}
         for half in halves:
             taps, centre = weights([pairs[c][half] for c in range(3)], 0.5 * time_step, half, lane)
             for field in fields:
-                value = 0.5 * (raw_ref[field, x + 5, half, tile + 2] + pairs[field][half]) + change(
-                    one_ref, field, x + 3, tile + 2, half, pairs[field], taps, centre, lane
-                )
-                values[field].append(closed(value, field, open_x, tile, half))
+                value = 0.5 * (
+                    raw_ref[field, x - raw_first, half, tile + 2] + pairs[field][half]
+                ) + change(one_ref, field, at, tile + 2, half, pairs[field], taps, centre, lane)
+                values[field].append(closed(value, field, is_open(x), tile, half))
         return values
 
-    for tile in range(tiles):
-        for half in halves:
-            sum_ref[half, tile] = jnp.zeros((8, 128), jnp.float32)
-        for half, value in enumerate(section_two(-1, tile, (0,), True)[0]):
-            below_ref[half, tile] = value
-
-    def plane(x, carry):
-        open_x = place_x * block_x + x != full_x - 1
-        waiting, previous = None, None
+    def plane(x, at, div_at, lifted_ref, smoke_ref, div_ref, ends_ref, hold_ref):
         for tile in range(tiles):
-            rows = pl.ds(3 + tile, 8, stride=5)
-            values = section_two(x, tile, (0, 1, 2, 3), open_x)
-            smoke = values[3]
+            values = section_two(x, tile, (0, 1, 2, 3))
+            for field in range(4):
+                for half in halves:
+                    hold_ref[field, half, tile] = values[field][half]
+        for tile in range(tiles):
+            rows = rows_of_tile(tile)
+            along_x, along_y, along_z, smoke = (
+                [hold_ref[field, half, tile] for half in halves] for field in range(4)
+            )
             along_z = [
-                values[2][half]
+                along_z[half]
                 + (time_step * buoyancy * 0.5)
                 * (smoke[half] + moved_along_z(smoke, half, 1, lane))
                 for half in halves
             ]
             along_z[1] = jnp.where(lane < 127, along_z[1], 0.0)
-            div = []
             for half in halves:
-                sum_ref[half, tile] = sum_ref[half, tile] + smoke[half]
+                ends_ref[1, half, tile] = ends_ref[1, half, tile] + smoke[half]
                 beneath = moved_along_z(along_z, half, -1, lane)
                 if half == 0:
                     beneath = jnp.where(lane > 0, beneath, 0.0)
-                div.append(
-                    values[0][half]
-                    - below_ref[half, tile]
+                below_y = hold_ref[1, half, (tile - 1) % tiles]
+                if tile == 0:
+                    below_y = pltpu.roll(below_y, 1, 0)
+                div_ref[div_at, half, rows, :] = (
+                    along_x[half]
+                    - ends_ref[0, half, tile]
                     + (along_z[half] - beneath)
-                    + values[1][half]
+                    + (along_y[half] - below_y)
                 )
-                below_ref[half, tile] = values[0][half]
-                lifted_ref[0, x, half, rows, :] = values[0][half]
-                lifted_ref[1, x, half, rows, :] = values[1][half]
-                lifted_ref[2, x, half, rows, :] = along_z[half]
-                smoke_ref[x, half, rows, :] = smoke[half]
-                if tile > 0:
-                    div_ref[x, half, rows, :] = div[half] - previous[half]
-            if tile == 0:
-                waiting = div
-            previous = values[1]
+                ends_ref[0, half, tile] = along_x[half]
+                lifted_ref[0, at, half, rows, :] = along_x[half]
+                lifted_ref[1, at, half, rows, :] = along_y[half]
+                lifted_ref[2, at, half, rows, :] = along_z[half]
+                smoke_ref[at, half, rows, :] = smoke[half]
+
+    return section_one, section_two, plane
+
+
+def fill_plane(stage_ref, at, velocity_ref, density_ref, x):
+    for field in range(4):
+        source = (velocity_ref[field, x] if field < 3 else density_ref[x]).astype(jnp.float32)
         for half in halves:
-            div_ref[x, half, pl.ds(3, 8, stride=5), :] = waiting[half] - pltpu.roll(
-                previous[half], 1, 0
-            )
+            stage_ref[field, at, half, 8:40, :] = source[:, half * 128 : half * 128 + 128]
+
+
+def fill_rims(stage_ref, at, low_y_ref, high_y_ref, pair):
+    for field in range(4):
+        for half in halves:
+            low, high = low_y_ref[field, pair, half], high_y_ref[field, pair, half]
+            stage_ref[field, at, half, 4:8, :] = low[0:4]
+            stage_ref[field, at + 1, half, 4:8, :] = low[4:8]
+            stage_ref[field, at, half, 40:44, :] = high[0:4]
+            stage_ref[field, at + 1, half, 40:44, :] = high[4:8]
+
+
+def fill_fifth(stage_ref, at, low_y_ref, x):
+    for half in halves:
+        stage_ref[1, at, half, 3:4, :] = low_y_ref[4, x // 8, half, x % 8 : x % 8 + 1, :]
+
+
+def spread(stage_ref, raw_ref, x):
+    for field in range(4):
+        for half in halves:
+            for tile in range(-2, tiles + 2):
+                raw_ref[field, x, half, tile + 2] = stage_ref[field, x, half, rows_of_tile(tile), :]
+
+
+def each(first, last, work):
+    def one(x, carry):
+        work(x)
         return carry
 
-    lax.fori_loop(0, block_x, plane, 0)
+    lax.fori_loop(first, last, one, 0)
+
+
+def inner_kernel(
+    velocity_hbm, density_hbm, low_y_ref, high_y_ref, one_hbm, lifted_hbm, smoke_hbm, div_hbm, ends_ref,
+    stage_ref, raw_ref, one_ref, lifted_ref, smoke_ref, div_ref, hold_ref, one_sent, plane_sent,
+    velocity_ref, density_ref, arrived,
+):
+    copies = fetched(velocity_hbm, density_hbm, velocity_ref, density_ref, arrived)
+    for copy in copies:
+        copy.start()
+    each(0, 8, lambda pair: fill_rims(stage_ref, 2 * pair, low_y_ref, high_y_ref, pair))
+    for x in range(block_x):
+        fill_fifth(stage_ref, x, low_y_ref, x)
+    for copy in copies:
+        copy.wait()
+    each(0, block_x, lambda x: fill_plane(stage_ref, x, velocity_ref, density_ref, x))
+    each(0, block_x, lambda x: spread(stage_ref, raw_ref, x))
+    section_one, _, plane = stencil(raw_ref, 0, one_ref, 2)
+    each(2, 14, section_one)
+    one_copies = [
+        pltpu.make_async_copy(
+            one_ref.at[:, 8 * part : 8 * part + 4], one_hbm.at[:, 4 * part : 4 * part + 4], one_sent.at[part]
+        )
+        for part in range(2)
+    ]
+    for copy in one_copies:
+        copy.start()
+    ends_ref[...] = jnp.zeros((2, 2, tiles, 8, 128), jnp.float32)
+
+    def plane_copies(at):
+        return (
+            pltpu.make_async_copy(lifted_ref.at[:, at], lifted_hbm.at[:, at], plane_sent.at[0, at]),
+            pltpu.make_async_copy(smoke_ref.at[at], smoke_hbm.at[at], plane_sent.at[1, at]),
+            pltpu.make_async_copy(div_ref.at[at], div_hbm.at[at], plane_sent.at[2, at]),
+        )
+
+    def work(at):
+        plane(at + 4, at, at, lifted_ref, smoke_ref, div_ref, ends_ref, hold_ref)
+        for copy in plane_copies(at):
+            copy.start()
+
+    each(0, 8, work)
+
+    def drain(at):
+        for copy in plane_copies(at):
+            copy.wait()
+
+    each(0, 8, drain)
+    for copy in one_copies:
+        copy.wait()
+
+
+def outer_kernel(
+    velocity_hbm, density_hbm, one_hbm, div_hbm, inner_ends_ref, low_x_ref, high_x_ref, low_y_ref,
+    high_y_ref, low_c_ref, high_c_ref, table_ref, lifted_ref, smoke_ref, out_ref,
+    stage_ref, raw_ref, one_ref, ends_ref, div_ref, freq_ref, total_ref, hold_ref, one_arrived,
+    velocity_ref, density_ref, arrived,
+):
+    copies = fetched(velocity_hbm, density_hbm, velocity_ref, density_ref, arrived)
+    inner_copies = [
+        pltpu.make_async_copy(
+            one_hbm.at[:, 4 * part : 4 * part + 4],
+            one_ref.at[:, 5 + 8 * part : 9 + 8 * part],
+            one_arrived.at[part],
+        )
+        for part in range(2)
+    ] + [pltpu.make_async_copy(div_hbm, div_ref.at[4:12], one_arrived.at[2])]
+    for copy in copies + inner_copies:
+        copy.start()
+    for field in range(4):
+        for x in range(4):
+            for half in halves:
+                for at, edge_ref, corner_ref in ((1, low_x_ref, low_c_ref), (21, high_x_ref, high_c_ref)):
+                    stage_ref[field, x + at, half, 8:40, :] = edge_ref[field * 4 + x, half]
+                    corner = corner_ref[field, x, half]
+                    stage_ref[field, x + at, half, 4:8, :] = corner[4:8]
+                    stage_ref[field, x + at, half, 40:44, :] = corner[0:4]
+    for half in halves:
+        stage_ref[0, 0, half, 8:40, :] = low_x_ref[16, half]
+    for pair in (0, 1, 6, 7):
+        fill_rims(stage_ref, 2 * pair + 5, low_y_ref, high_y_ref, pair)
+    for x in (0, 1, 2, 3, 12, 13, 14, 15):
+        fill_fifth(stage_ref, x + 5, low_y_ref, x)
+    for copy in copies:
+        copy.wait()
+
+    def fill(at):
+        x = jnp.where(at < 4, at, at + 8)
+        fill_plane(stage_ref, x + 5, velocity_ref, density_ref, x)
+
+    each(0, 8, fill)
+    section_one, section_two, plane = stencil(raw_ref, -5, one_ref, -3)
+
+    each(0, 17, lambda at: spread(stage_ref, raw_ref, jnp.where(at < 9, at, at + 8)))
+    section_one(-3, (0,))
+    each(0, 8, lambda at: section_one(jnp.where(at < 4, at - 2, at + 10)))
+    for copy in inner_copies:
+        copy.wait()
+    for tile in range(tiles):
+        for half, value in enumerate(section_two(-1, tile, (0,))[0]):
+            ends_ref[0, half, tile] = value
+    ends_ref[1] = inner_ends_ref[1]
+    each(0, 4, lambda x: plane(x, x, x, lifted_ref, smoke_ref, div_ref, ends_ref, hold_ref))
     for tile in range(tiles):
         for half in halves:
-            total_ref[half, pl.ds(3 + tile, 8, stride=5), :] = sum_ref[half, tile]
+            rows = rows_of_tile(tile)
+            div_ref[4, half, rows, :] = div_ref[4, half, rows, :] - ends_ref[0, half, tile]
+    ends_ref[0] = inner_ends_ref[0]
+    each(12, 16, lambda x: plane(x, x - 8, x, lifted_ref, smoke_ref, div_ref, ends_ref, hold_ref))
+    for tile in range(tiles):
+        for half in halves:
+            total_ref[half, rows_of_tile(tile), :] = ends_ref[1, half, tile]
     lines = [div_ref[:, half, 8:40, :].reshape(block_x * block_y, 128) for half in halves]
     freq_ref[...] = dot(jnp.concatenate(lines, axis=1), table_ref[...], ((1,), (0,)))
 
-    def pack(x, carry):
-        for part in range(4):
-            for half in halves:
-                tile = freq_ref[
-                    pl.ds(pl.multiple_of(x * block_y, 8) + part * 8, 8), half * 128 : half * 128 + 128
-                ]
-                out_ref[pl.ds(half * 8 * send_rows + part * 16 + x, 8, stride=send_rows), :] = (
-                    turn_groups(tile)
-                )
-        return carry
-
-    lax.fori_loop(0, block_x, pack, 0)
+    def pack(step):
+        for x in range(4):
+            x = step * 4 + x
+            for part in range(4):
+                for half in halves:
+                    tile = freq_ref[
+                        pl.ds(pl.multiple_of(x * block_y, 8) + part * 8, 8),
+                        half * 128 : half * 128 + 128,
+                    ]
+                    out_ref[
+                        pl.ds(half * 8 * send_rows + part * 16 + x, 8, stride=send_rows), :
+                    ] = turn_groups(tile)
+
+    each(0, block_x // 4, pack)
     for part in range(4):
         for half in halves:
             tile = total_ref[half, 8 + part * 8 : 16 + part * 8, :]
@@ -389,9 +472,8 @@
     eigen_ref, got_ref, eigen_x_ref, table_ref, local_ref, ends_ref, send_ref, before_ref, line_ref
 ):
     place_x, place_y = lax.axis_index("gx"), lax.axis_index("gy")
-    for part in range(4):
-        lines = got_ref[:, part * 16 : part * 16 + 16, :].reshape(full_x, 128)
-        line_ref[part * 128 : part * 128 + 128, :] = dot(lines, table_ref[...], ((0,), (0,)))
+    lines = [got_ref[:, part * 16 : part * 16 + 16, :].reshape(full_x, 128) for part in range(4)]
+    line_ref[...] = dot(jnp.concatenate(lines, axis=1), table_ref[...], ((0,), (0,)))
     lam = eigen_sum(eigen_ref, eigen_x_ref, place_x)
     rho, _ = roots_of(lam)
     special = lam == 0.0
@@ -426,7 +508,7 @@
 
 
 def backward_kernel(
-    eigen_ref, local_ref, ends_ref, got_ref, eigen_x_ref, table_ref, next_ref, before_ref, out_ref, line_ref
+    eigen_ref, local_ref, ends_ref, got_ref, eigen_x_ref, table_ref, before_ref, out_ref, line_ref
 ):
     place_x, place_y = lax.axis_index("gx"), lax.axis_index("gy")
     lam = eigen_sum(eigen_ref, eigen_x_ref, place_x)
@@ -469,20 +551,20 @@
         line_ref[rows, :] = jnp.where(special, level, scale * (here + enter_low))
         level = level + (here + flux_in - mean * (y + 1.0))
     line_ref[(block_y + 1) * 16 :, :] = jnp.zeros((112, full_x), jnp.float32)
+    found = dot(table_ref[...], line_ref[...], ((1,), (1,)))
     for part in range(5):
-        lines = line_ref[part * 128 : part * 128 + 128, :]
-        out_ref[:, part * 16 : part * 16 + 16, :] = dot(table_ref[...], lines, ((1,), (1,))).reshape(
-            count_x, block_x, 128
-        )
+        lanes = slice(part * 128, part * 128 + 128)
+        out_ref[:, part * 16 : part * 16 + 16, :] = found[:, lanes].reshape(count_x, block_x, 128)
         if part < 4:
-            out_ref[:, 80 + part : 81 + part, :] = dot(next_ref[...], lines, ((1,), (1,))).reshape(
-                count_x, 1, 128
-            )
+            for peer in range(count_x - 1):
+                at = (peer + 1) * block_x
+                out_ref[peer, 80 + part : 81 + part, :] = found[at : at + 1, lanes]
+            out_ref[count_x - 1, 80 + part : 81 + part, :] = jnp.zeros((1, 128), jnp.float32)
     out_ref[:, 84:88, :] = before_ref[:, 0:4, :]
 
 
 def final_kernel(
-    got_ref, lifted_ref, smoke_ref, table_ref, out_hbm, glow_hbm,
+    got_ref, lifted_ref, lifted_in_ref, smoke_ref, smoke_in_ref, table_ref, out_hbm, glow_hbm,
     freq_ref, press_ref, out_ref, glow_ref, out_sent, glow_sent,
 ):
     place_x, place_y = lax.axis_index("gx"), lax.axis_index("gy")
@@ -511,8 +593,8 @@
     def whole(ref, *at):
         return jnp.concatenate([ref[(*at, half, slice(8, 40))] for half in range(2)], axis=1)
 
-    def shine(x, running):
-        smoke = whole(smoke_ref, x)
+    def shine(ref, shift, x, running):
+        smoke = whole(ref, x - shift)
         depth = attenuation * smoke
         series = 1.0 - depth * (1.0 / 7.0)
         for order in (6.0, 5.0, 4.0, 3.0, 2.0):
@@ -522,17 +604,21 @@
         glow_copy(x).start()
         return running + smoke
 
-    lax.fori_loop(0, block_x, shine, entered)
-
-    def one(x, carry):
-        for part in range(5):
-            for half in range(2):
-                freq_ref[x, part * 8 : part * 8 + 8, half * 128 : half * 128 + 128] = tile_at(
-                    part * 16 + x, half
-                )
-        return carry
-
-    lax.fori_loop(0, block_x, one, 0)
+    parts = ((0, 4, 0, lifted_ref, smoke_ref), (4, 12, 4, lifted_in_ref, smoke_in_ref),
+             (12, 16, 8, lifted_ref, smoke_ref))
+    for first, last, shift, _, ref in parts:
+        entered = lax.fori_loop(first, last, functools.partial(shine, ref, shift), entered)
+
+    def unpack(step):
+        for x in range(4):
+            x = step * 4 + x
+            for part in range(5):
+                for half in range(2):
+                    freq_ref[x, part * 8 : part * 8 + 8, half * 128 : half * 128 + 128] = tile_at(
+                        part * 16 + x, half
+                    )
+
+    each(0, block_x // 4, unpack)
     for part in range(4):
         for half in range(2):
             freq_ref[block_x, part * 8 : part * 8 + 8, half * 128 : half * 128 + 128] = tile_at(
@@ -547,22 +633,29 @@
     open_y = along_y < full_y - 1
     open_z = along_z < size_z - 1
 
-    def finish(x, carry):
-        here = press_ref[x, 0:block_y, :]
-        open_x = place_x * block_x + x < full_x - 1
-        out_ref[x, 0] = jnp.where(
-            open_x, whole(lifted_ref, 0, x) - (press_ref[x + 1, 0:block_y, :] - here), 0.0
-        )
-        out_ref[x, 1] = jnp.where(
-            open_y, whole(lifted_ref, 1, x) - (press_ref[x, 1 : block_y + 1, :] - here), 0.0
-        )
-        out_ref[x, 2] = jnp.where(
-            open_z, whole(lifted_ref, 2, x) - (pltpu.roll(here, size_z - 1, 1) - here), 0.0
-        )
-        out_copy(x).start()
-        return carry
-
-    lax.fori_loop(0, block_x, finish, 0)
+    def finish(ref, shift, first):
+        for x in range(first, first + 4):
+            here = press_ref[x, 0:block_y, :]
+            open_x = place_x * block_x + x < full_x - 1
+            out_ref[x, 0] = jnp.where(
+                open_x, whole(ref, 0, x - shift) - (press_ref[x + 1, 0:block_y, :] - here), 0.0
+            )
+            out_ref[x, 1] = jnp.where(
+                open_y, whole(ref, 1, x - shift) - (press_ref[x, 1 : block_y + 1, :] - here), 0.0
+            )
+            out_ref[x, 2] = jnp.where(
+                open_z, whole(ref, 2, x - shift) - (pltpu.roll(here, size_z - 1, 1) - here), 0.0
+            )
+        for x in range(first, first + 4):
+            out_copy(x).start()
+
+    for first, ref, shift in (
+        (0, lifted_ref, 0),
+        (4, lifted_in_ref, 4),
+        (8, lifted_in_ref, 4),
+        (12, lifted_ref, 8),
+    ):
+        finish(ref, shift, first)
 
     def drain(x, carry):
         glow_copy(x).wait()
@@ -576,7 +669,7 @@
     return jax.ShapeDtypeStruct(dims, jnp.float32)
 
 
-def call(kernel, outs, scratch, grant, spaces={}, outside=False):
+def call(kernel, outs, scratch, grant, spaces={}, outside=0):
     vmem = pl.BlockSpec(memory_space=pltpu.VMEM)
 
     def run(*args):
@@ -584,12 +677,15 @@
             pl.BlockSpec(memory_space=spaces[at]) if at in spaces else vmem
             for at in range(len(args))
         ]
-        place = pl.BlockSpec(memory_space=pltpu.HBM) if outside else vmem
+        places = [
+            pl.BlockSpec(memory_space=pltpu.HBM) if at < outside else vmem
+            for at in range(len(jax.tree.leaves(outs)))
+        ]
         return pl.pallas_call(
             kernel,
             out_shape=outs,
             in_specs=specs,
-            out_specs=jax.tree.map(lambda _: place, outs),
+            out_specs=jax.tree.unflatten(jax.tree.structure(outs), places),
             scratch_shapes=[
                 pltpu.VMEM(entry, jnp.float32) if isinstance(entry, tuple) else entry
                 for entry in scratch
@@ -620,32 +716,57 @@
 def step(velocity, density, rims):
     table_z = cosine_array(size_z)
     table_x = cosine_array(full_x)
-    next_x = np.concatenate(
-        [table_x.T[block_x::block_x], np.zeros((1, full_x), np.float32)], axis=0
-    )
     eigen_z = jnp.asarray(eigen_array(size_z))
     eigen_x = jnp.asarray(np.broadcast_to(eigen_array(full_x)[None, :], (chunk_z, full_x)))
-    lifted, smoke, packed = call(
-        advect_kernel,
+    low_x, high_x, low_y, high_y, low_c, high_c = rims
+    here = {0: pltpu.HBM, 1: pltpu.HBM, 2: pltpu.HBM, 3: pltpu.HBM}
+    thick, plane = (2, 9, 8, 128), (2, 48, 128)
+    one, lifted_in, smoke_in, div_in, ends = call(
+        inner_kernel,
         (
-            shaped(3, block_x, 2, 48, 128),
-            shaped(block_x, 2, 48, 128),
-            shaped(count_x * send_rows, 128),
+            shaped(4, 8, *thick),
+            shaped(3, 8, *plane),
+            shaped(8, *plane),
+            shaped(8, *plane),
+            shaped(2, 2, tiles, 8, 128),
         ),
         [
-            (4, block_x + 9, 2, 48, 128),
-            (4, block_x + 9, 2, 9, 8, 128),
-            (4, block_x + 5, 2, 9, 8, 128),
-            (2, tiles, 8, 128),
-            (block_x, 2, 48, 128),
+            (4, block_x, *plane),
+            (4, block_x, *thick),
+            (4, 12, *thick),
+            (3, 8, *plane),
+            (8, *plane),
+            (8, *plane),
+            (4, 2, tiles, 8, 128),
+            pltpu.SemaphoreType.DMA((2,)),
+            pltpu.SemaphoreType.DMA((3, 8)),
+            *inputs_here,
+        ],
+        20,
+        {0: pltpu.HBM, 1: pltpu.HBM},
+        outside=4,
+    )(velocity, density, low_y, high_y)
+    lifted, smoke, packed = call(
+        outer_kernel,
+        (shaped(3, 8, *plane), shaped(8, *plane), shaped(count_x * send_rows, 128)),
+        [
+            (4, block_x + 9, *plane),
+            (4, block_x + 9, *thick),
+            (4, block_x + 5, *thick),
+            (2, 2, tiles, 8, 128),
+            (block_x, *plane),
             (block_x * block_y, size_z),
-            (2, tiles, 8, 128),
-            (2, 48, 128),
+            plane,
+            (4, 2, tiles, 8, 128),
+            pltpu.SemaphoreType.DMA((3,)),
             *inputs_here,
         ],
         25,
-        {0: pltpu.HBM, 1: pltpu.HBM},
-    )(velocity, density, *rims, jnp.asarray(np.ascontiguousarray(table_z.T[:, turned])))
+        here,
+    )(
+        velocity, density, one, div_in, ends, low_x, high_x, low_y, high_y, low_c, high_c,
+        jnp.asarray(np.ascontiguousarray(table_z.T[:, turned])),
+    )
     got = lax.all_to_all(
         packed.reshape(count_x, send_rows, 128), "gx", split_axis=0, concat_axis=0, tiled=True
     )
@@ -669,7 +790,7 @@
         [(5 * 128, full_x)],
         4,
         {0: pltpu.SMEM},
-    )(eigen_z, local, ends, moments, eigen_x, table_xt, jnp.asarray(next_x), before)
+    )(eigen_z, local, ends, moments, eigen_x, table_xt, before)
     back = lax.all_to_all(back, "gx", split_axis=0, concat_axis=0, tiled=True)
     return call(
         final_kernel,
@@ -683,8 +804,11 @@
             pltpu.SemaphoreType.DMA((block_x,)),
         ],
         8,
-        outside=True,
-    )(back.reshape(count_x * back_rows, 128), lifted, smoke, jnp.asarray(table_z))
+        outside=2,
+    )(
+        back.reshape(count_x * back_rows, 128), lifted, lifted_in, smoke, smoke_in,
+        jnp.asarray(table_z),
+    )
 
 
 def moved(part, axis, upward):
@@ -700,7 +824,10 @@
         inputs_here,
         4,
         {0: pltpu.HBM, 1: pltpu.HBM},
-    )(velocity, density)
+    )(
+        pltpu.with_memory_space_constraint(velocity, pltpu.HBM),
+        pltpu.with_memory_space_constraint(density, pltpu.HBM),
+    )
     low_x = moved(up_x, "gx", True)
     high_x = moved(down_x, "gx", False)
     low_y = moved(up_y, "gy", True)

time: 116 us -> 106 us (0.914)
  waiting for transfers between devices: 10.5 us -> 6.07 us
  local copies, waits for them, and re-layouts: 2.12 us -> 0.04 us
  blocking collectives: 59 us -> 57.4 us
  Pallas kernels: 25.6 us -> 24.2 us
    ppermute x6, waiting for transfers between devices: 10.5 us -> 6.07 us  [moved(): return lax.ppermute(part, axis, pairs)]
    unnamed x18 -> x12, local copies, waits for them, and re-layouts: 2.12 us -> 0.04 us
    all_to_all x1, blocking collectives: 20 us -> 18.2 us  [step(): lax.all_to_all(packed.reshape(count_x, send_rows, 128), 'gx', split_axis=...]
    pallas_call x6 -> x7, Pallas kernels: 25.6 us -> 24.2 us  [run(): pl.pallas_call(kernel, out_shape=outs, in_specs=specs, out_specs=jax.tree...]
  transfers between devices with their start and end apart: 6 -> 6, of which waited for: 3 -> 1; matrix products, arithmetic and copies ran while one was open for 0% -> 0% of each run, Pallas kernels for 0% -> 8%
where the time goes in v1:
time: 106 us
  blocking collectives  57.4 us (54%)
  Pallas kernels  24.2 us (23%)
  starting transfers between devices  17.2 us (16%)
  waiting for transfers between devices  6.07 us (6%)
    pallas_call x7, Pallas kernels, run(): pl.pallas_call(kernel, out_shape=outs, in_specs=specs, out_specs=jax.tree...  24.2 us
    all_to_all x1, blocking collectives, step(): lax.all_to_all(moments, 'gy', split_axis=0, concat_axis=0, tiled=True)  22.8 us
    all_to_all x1, blocking collectives, step(): lax.all_to_all(packed.reshape(count_x, send_rows, 128), 'gx', split_axis=...  18.2 us
    ppermute x6, starting transfers between devices, moved(): return lax.ppermute(part, axis, pairs)  17.2 us
    all_to_all x1, blocking collectives, step(): back = lax.all_to_all(back, 'gx', split_axis=0, concat_axis=0, tiled=True)  16.3 us
    ppermute x6, waiting for transfers between devices, moved(): return lax.ppermute(part, axis, pairs)  6.07 us
  transfers between devices with their start and end apart: 6, of which 1 were waited for; matrix products, arithmetic and copies ran while one was open for 0% of the time, Pallas kernels for 8%

profile of v1, /device:TPU:1, one launch (start us, length us, event | category | flops | bytes accessed | tf_op | source)
XLA Modules:
  0.0 105.7 jit_solution(17331716921142768322)
XLA Ops:
  0.6 1.3 %shard_map.86 = (f32[17,2,32,128]{3,2,1,0:T(8,128)S(1)}, f32[16,2,32,128]{3,2,1,0:T(8,128)S(1)}, f32[5,8,2,8,128]{4,3,2,1,0:T(8,128)S(1)}, f32[4,8,2,8,128]{4,3,2,1,0:T(8,128)S(1)}) custom-call(bf16[3,16,32,256]{3,2,1,0:T(8,128)(2,1)} %velocity_hbm.5, bf16[16,32,256]{2,1,0:T(8,128)(2,1)} %density_hbm.5), custom_call_target="tpu_custom_call" | custom-call | flops 1000000000 | bytes 1024 | tf_op jit(solution)/shard_map/pallas_call | solution.py:684
  2.0 4.1 %collective-permute-start.2 = (f32[17,2,32,128]{3,2,1,0:T(8,128)S(1)}, f32[17,2,32,128]{3,2,1,0:T(8,128)S(1)}, u32[]{:S(2)}, u32[]{:S(2)}) collective-permute-start(f32[17,2,32,128]{3,2,1,0:T(8,128)S(1)} %get-tuple-element.25), channel_id=1, source_target_pairs={{0,16},{16,32},{32,48},{48,64},{64,80},{80,96},{96,112},{112,128},... | collective-permute-start | bytes 1671176 | tf_op jit(solution)/shard_map/ppermute | solution.py:816
  6.0 4.4 %collective-permute-start = (f32[5,8,2,8,128]{4,3,2,1,0:T(8,128)S(1)}, f32[5,8,2,8,128]{4,3,2,1,0:T(8,128)S(1)}, u32[]{:S(2)}, u32[]{:S(2)}) collective-permute-start(f32[5,8,2,8,128]{4,3,2,1,0:T(8,128)S(1)} %get-tuple-element.20), channel_id=1, source_target_pairs={{0,1},{1,2},{2,3},{3,4},{4,5},{5,6},{6,7},{7,8},{8,9},{9,10},{10,1... | collective-permute-start | bytes 983048 | tf_op jit(solution)/shard_map/ppermute | solution.py:816
  10.4 1.3 %collective-permute-start.3 = (f32[16,2,32,128]{3,2,1,0:T(8,128)S(1)}, f32[16,2,32,128]{3,2,1,0:T(8,128)S(1)}, u32[]{:S(2)}, u32[]{:S(2)}) collective-permute-start(f32[16,2,32,128]{3,2,1,0:T(8,128)S(1)} %get-tuple-element.26), channel_id=1, source_target_pairs={{16,0},{32,16},{48,32},{64,48},{80,64},{96,80},{112,96},{128,112},... | collective-permute-start | bytes 1572872 | tf_op jit(solution)/shard_map/ppermute | solution.py:816
  11.7 0.0 copy-start
  11.7 0.0 copy-start.1
  11.7 2.1 %collective-permute-start.1 = (f32[4,8,2,8,128]{4,3,2,1,0:T(8,128)S(1)}, f32[4,8,2,8,128]{4,3,2,1,0:T(8,128)S(1)}, u32[]{:S(2)}, u32[]{:S(2)}) collective-permute-start(f32[4,8,2,8,128]{4,3,2,1,0:T(8,128)S(1)} %get-tuple-element.21), channel_id=1, source_target_pairs={{1,0},{2,1},{3,2},{4,3},{5,4},{6,5},{7,6},{8,7},{9,8},{10,9},{11,1... | collective-permute-start | bytes 786440 | tf_op jit(solution)/shard_map/ppermute | solution.py:816
  13.8 6.1 %collective-permute-done.1.high_y_ref = f32[4,8,2,8,128]{4,3,2,1,0:T(8,128)S(1)} collective-permute-done((f32[4,8,2,8,128]{4,3,2,1,0:T(8,128)S(1)}, f32[4,8,2,8,128]{4,3,2,1,0:T(8,128)S(1)}, u32[]{:S(2)}, u32[]{:S(2)}) %collective-permute-start.1) | collective-permute-done | bytes 262176 | tf_op jit(solution)/shard_map/ppermute | solution.py:816
  19.9 0.0 collective-permute-done.low_y_ref
  19.9 4.0 %collective-permute-start.4 = (f32[4,4,2,8,128]{4,3,2,1,0:T(8,128)S(1)}, f32[4,4,2,8,128]{4,3,2,1,0:T(8,128)S(1)}, u32[]{:S(2)}, u32[]{:S(2)}) collective-permute-start(f32[4,4,2,8,128]{4,3,2,1,0:T(8,128)S(1)} %get-tuple-element.27), channel_id=1, source_target_pairs={{0,16},{16,32},{32,48},{48,64},{64,80},{80,96},{96,112},{112,128},... | collective-permute-start | bytes 393224 | tf_op jit(solution)/shard_map/ppermute | solution.py:816
  23.9 0.0 copy-start.3
  23.9 1.4 %collective-permute-start.5 = (f32[4,4,2,8,128]{4,3,2,1,0:T(8,128)S(1)}, f32[4,4,2,8,128]{4,3,2,1,0:T(8,128)S(1)}, u32[]{:S(2)}, u32[]{:S(2)}) collective-permute-start(f32[4,4,2,8,128]{4,3,2,1,0:T(8,128)S(1)} %get-tuple-element.28), channel_id=1, source_target_pairs={{16,0},{32,16},{48,32},{64,48},{80,64},{96,80},{112,96},{128,112},... | collective-permute-start | bytes 393224 | tf_op jit(solution)/shard_map/ppermute | solution.py:816
  25.3 0.0 copy-done
  25.3 0.0 copy-done.1
  25.4 8.5 %shard_map.87 = (f32[4,8,2,9,8,128]{5,4,3,2,1,0:T(8,128)S(1)}, f32[3,8,2,48,128]{4,3,2,1,0:T(8,128)S(1)}, f32[8,2,48,128]{3,2,1,0:T(8,128)S(1)}, f32[8,2,48,128]{3,2,1,0:T(8,128)S(1)}, f32[2,2,5,8,128]{4,3,2,1,0:T(8,128)S(1)}) custom-call(bf16[3,16,32,256]{3,2,1,0:T(8,128)(2,1)S(1)} %copy-done, bf16[16,32,256]{2,1,0:T(8,128)(2,1)S(1)} %copy-done.1, ...), custom_call_target="tpu_custom_call" | custom-call | flops 1000000000 | bytes 1024 | tf_op jit(solution)/shard_map/pallas_call | solution.py:684
  33.9 0.0 collective-permute-done.4.low_c_ref
  33.9 0.0 collective-permute-done.5.high_c_ref
  33.9 0.0 collective-permute-done.3.high_x_ref
  33.9 0.0 collective-permute-done.2.low_x_ref
  33.9 0.0 copy-done.3
  33.9 0.0 copy-start.4
  34.0 0.0 copy-start.5
  34.0 7.7 %shard_map.89 = (f32[3,8,2,48,128]{4,3,2,1,0:T(8,128)S(1)}, f32[8,2,48,128]{3,2,1,0:T(8,128)S(1)}, f32[1152,128]{1,0:T(8,128)S(1)}) custom-call(bf16[3,16,32,256]{3,2,1,0:T(8,128)(2,1)S(1)} %copy-done, bf16[16,32,256]{2,1,0:T(8,128)(2,1)S(1)} %copy-done.1, f32[4,8,2,9,8,128]{5,4,3,2,1,0:T(8,128)S(1)} %get-tuple-element.22.one_hbm, ...), custom_call_target="tpu_custom_call" | custom-call | flops 1000000000 | bytes 1024 | tf_op jit(solution)/shard_map/pallas_call | solution.py:684
  41.7 18.2 %all_to_all.15.got_ref = f32[16,72,128]{2,1,0:T(8,128)S(1)} all-to-all(f32[16,72,128]{2,1,0:T(8,128)S(1)} %bitcast.3), channel_id=1, replica_groups=mesh['gx'=16,'gy'=16] {'gx'}, dimensions={0} | all-to-all | bytes 1179648 | tf_op jit(solution)/shard_map/all_to_all | solution.py:770
  59.9 0.0 copy-done.4
  59.9 0.0 copy-done.5
  59.9 1.3 %shard_map.90 = (f32[512,256]{1,0:T(8,128)S(1)}, f32[2,16,256]{2,1,0:T(8,128)S(1)}, f32[16,16,256]{2,1,0:T(8,128)S(1)}, f32[16,8,128]{2,1,0:T(8,128)S(1)}) custom-call(f32[256]{0:T(256)S(1)} %copy-done.4, f32[16,72,128]{2,1,0:T(8,128)S(1)} %all_to_all.15.got_ref, f32[16,256]{1,0:T(8,128)S(1)} %jit_solution_.3.eigen_x_ref, f32[256,256]{1,0:T(8,128)S(1)} %copy-done.5), custom_call_target="tpu_custom_call" | custom-call | flops 1000000000 | bytes 1024 | tf_op jit(solution)/shard_map/pallas_call | solution.py:684
  61.2 22.8 %all_to_all.16.got_ref = f32[16,16,256]{2,1,0:T(8,128)S(1)} all-to-all(f32[16,16,256]{2,1,0:T(8,128)S(1)} %get-tuple-element.32), channel_id=1, replica_groups=mesh['gx'=16,'gy'=16] {'gy'}, dimensions={0} | all-to-all | bytes 524288 | tf_op jit(solution)/shard_map/all_to_all | solution.py:786
  84.0 1.6 %shard_map.91 = f32[16,88,128]{2,1,0:T(8,128)S(1)} custom-call(f32[256]{0:T(256)S(1)} %copy-done.4, f32[512,256]{1,0:T(8,128)S(1)} %get-tuple-element.30.local_ref, f32[2,16,256]{2,1,0:T(8,128)S(1)} %get-tuple-element.31.ends_ref, f32[16,16,256]{2,1,0:T(8,128)S(1)} %all_to_all.16.got_ref, f32[16,256]{1,0:T(8,128)S(1)} %jit_solution_.3.eigen_x_ref, ...), custom_call_target="tpu_custom_call" | custom-call | flops 1000000000 | bytes 1024 | tf_op jit(solution)/shard_map/pallas_call | solution.py:684
  85.6 0.0 copy-start.2
  85.7 16.3 %all_to_all.17 = f32[16,88,128]{2,1,0:T(8,128)S(1)} all-to-all(f32[16,88,128]{2,1,0:T(8,128)S(1)} %shard_map.91), channel_id=1, replica_groups=mesh['gx'=16,'gy'=16] {'gx'}, dimensions={0} | all-to-all | bytes 1441792 | tf_op jit(solution)/shard_map/all_to_all | solution.py:794
  102.0 0.0 copy-done.2
  102.0 3.7 %shard_map.92 = (f32[3,16,32,256]{3,2,1,0:T(8,128)}, f32[16,32,256]{2,1,0:T(8,128)}) custom-call(f32[1408,128]{1,0:T(8,128)S(1)} %bitcast.2, f32[3,8,2,48,128]{4,3,2,1,0:T(8,128)S(1)} %get-tuple-element.34.lifted_ref, f32[3,8,2,48,128]{4,3,2,1,0:T(8,128)S(1)} %get-tuple-element.35.lifted_in_ref, f32[8,2,48,128]{3,2,1,0:T(8,128)S(1)} %get-tuple-element.36.smoke_ref, ...), custom_call_target="tpu_custom_call" | custom-call | flops 1000000000 | bytes 1024 | tf_op jit(solution)/shard_map/pallas_call | solution.py:684
  (2 shorter events, 0.0 us)
Async XLA Ops:
  2.0 32.0 %collective-permute-start.2 = (f32[17,2,32,128]{3,2,1,0:T(8,128)S(1)}, f32[17,2,32,128]{3,2,1,0:T(8,128)S(1)}, u32[]{:S(2)}, u32[]{:S(2)}) collective-permute-start(f32[17,2,32,128]{3,2,1,0:T(8,128)S(1)} %get-tuple-element.25), channel_id=1, source_target_pairs={{0,16},{16,32},{32,48},{48,64},{64,80},{80,96},{96,112},{112,128},... | collective-permute-start | bytes 1671176 | tf_op jit(solution)/shard_map/ppermute | solution.py:816
  6.0 13.8 %collective-permute-start = (f32[5,8,2,8,128]{4,3,2,1,0:T(8,128)S(1)}, f32[5,8,2,8,128]{4,3,2,1,0:T(8,128)S(1)}, u32[]{:S(2)}, u32[]{:S(2)}) collective-permute-start(f32[5,8,2,8,128]{4,3,2,1,0:T(8,128)S(1)} %get-tuple-element.20), channel_id=1, source_target_pairs={{0,1},{1,2},{2,3},{3,4},{4,5},{5,6},{6,7},{7,8},{8,9},{9,10},{10,1... | collective-permute-start | bytes 983048 | tf_op jit(solution)/shard_map/ppermute | solution.py:816
  10.4 23.5 %collective-permute-start.3 = (f32[16,2,32,128]{3,2,1,0:T(8,128)S(1)}, f32[16,2,32,128]{3,2,1,0:T(8,128)S(1)}, u32[]{:S(2)}, u32[]{:S(2)}) collective-permute-start(f32[16,2,32,128]{3,2,1,0:T(8,128)S(1)} %get-tuple-element.26), channel_id=1, source_target_pairs={{16,0},{32,16},{48,32},{64,48},{80,64},{96,80},{112,96},{128,112},... | collective-permute-start | bytes 1572872 | tf_op jit(solution)/shard_map/ppermute | solution.py:816
  11.7 13.6 %copy-start = (bf16[3,16,32,256]{3,2,1,0:T(8,128)(2,1)S(1)}, bf16[3,16,32,256]{3,2,1,0:T(8,128)(2,1)}, u32[]{:S(2)}) copy-start(bf16[3,16,32,256]{3,2,1,0:T(8,128)(2,1)} %velocity_hbm.5) | copy-start | bytes 2359300
  11.7 13.6 %copy-start.1 = (bf16[16,32,256]{2,1,0:T(8,128)(2,1)S(1)}, bf16[16,32,256]{2,1,0:T(8,128)(2,1)}, u32[]{:S(2)}) copy-start(bf16[16,32,256]{2,1,0:T(8,128)(2,1)} %density_hbm.5) | copy-start | bytes 786436
  11.7 8.1 %collective-permute-start.1 = (f32[4,8,2,8,128]{4,3,2,1,0:T(8,128)S(1)}, f32[4,8,2,8,128]{4,3,2,1,0:T(8,128)S(1)}, u32[]{:S(2)}, u32[]{:S(2)}) collective-permute-start(f32[4,8,2,8,128]{4,3,2,1,0:T(8,128)S(1)} %get-tuple-element.21), channel_id=1, source_target_pairs={{1,0},{2,1},{3,2},{4,3},{5,4},{6,5},{7,6},{8,7},{9,8},{10,9},{11,1... | collective-permute-start | bytes 786440 | tf_op jit(solution)/shard_map/ppermute | solution.py:816
  19.9 14.0 %collective-permute-start.4 = (f32[4,4,2,8,128]{4,3,2,1,0:T(8,128)S(1)}, f32[4,4,2,8,128]{4,3,2,1,0:T(8,128)S(1)}, u32[]{:S(2)}, u32[]{:S(2)}) collective-permute-start(f32[4,4,2,8,128]{4,3,2,1,0:T(8,128)S(1)} %get-tuple-element.27), channel_id=1, source_target_pairs={{0,16},{16,32},{32,48},{48,64},{64,80},{80,96},{96,112},{112,128},... | collective-permute-start | bytes 393224 | tf_op jit(solution)/shard_map/ppermute | solution.py:816
  23.9 10.0 %copy-start.3 = (f32[256,256]{1,0:T(8,128)S(1)}, f32[256,256]{1,0:T(8,128)}, u32[]{:S(2)}) copy-start(f32[256,256]{1,0:T(8,128)} %constant.10.clone.table_ref) | copy-start | bytes 786436
  23.9 10.0 %collective-permute-start.5 = (f32[4,4,2,8,128]{4,3,2,1,0:T(8,128)S(1)}, f32[4,4,2,8,128]{4,3,2,1,0:T(8,128)S(1)}, u32[]{:S(2)}, u32[]{:S(2)}) collective-permute-start(f32[4,4,2,8,128]{4,3,2,1,0:T(8,128)S(1)} %get-tuple-element.28), channel_id=1, source_target_pairs={{16,0},{32,16},{48,32},{64,48},{80,64},{96,80},{112,96},{128,112},... | collective-permute-start | bytes 393224 | tf_op jit(solution)/shard_map/ppermute | solution.py:816
  33.9 25.9 %copy-start.4 = (f32[256]{0:T(256)S(1)}, f32[256]{0:T(256)}, u32[]{:S(2)}) copy-start(f32[256]{0:T(256)} %constant.8.clone.eigen_ref) | copy-start | bytes 3076
  34.0 25.9 %copy-start.5 = (f32[256,256]{1,0:T(8,128)S(1)}, f32[256,256]{1,0:T(8,128)}, u32[]{:S(2)}) copy-start(f32[256,256]{1,0:T(8,128)} %constant.11.clone.table_ref) | copy-start | bytes 786436
  85.6 16.4 %copy-start.2 = (f32[256,256]{1,0:T(8,128)S(1)}, f32[256,256]{1,0:T(8,128)}, u32[]{:S(2)}) copy-start(f32[256,256]{1,0:T(8,128)} %constant.12.clone.table_ref) | copy-start | bytes 786436

commit v2 on v1

--- a/solution.py
+++ b/solution.py
@@ -11,7 +11,6 @@
 time_step = 0.4
 buoyancy = 2.0
 extinction = 3.0
-highest = lax.Precision.HIGHEST
 
 block_x, block_y, size_z = 16, 32, 256
 count_x, count_y = 16, 16
@@ -55,10 +54,29 @@
 turned = [half * 128 + (-group % 8) * 16 + mode for half in range(2) for group in range(8) for mode in range(16)]
 
 
+def parts_of(value, count):
+    found = []
+    for _ in range(count):
+        found.append(value.astype(jnp.bfloat16))
+        value = value - found[-1].astype(np.float32)
+    return found
+
+
+pairs_of = {2: ((0, 0), (0, 1), (1, 0)), 3: ((0, 0), (0, 1), (1, 0), (0, 2), (2, 0), (1, 1))}
+
+
+def data_side(value, axis, count):
+    found = parts_of(value, count)
+    return jnp.concatenate([found[at] for at, _ in pairs_of[count]], axis=axis)
+
+
+def table_side(table, axis, count):
+    found = parts_of(table, count)
+    return jnp.asarray(np.concatenate([found[at] for _, at in pairs_of[count]], axis=axis))
+
+
 def dot(left, right, dims):
-    return lax.dot_general(
-        left, right, (dims, ((), ())), precision=highest, preferred_element_type=jnp.float32
-    )
+    return lax.dot_general(left, right, (dims, ((), ())), preferred_element_type=jnp.float32)
 
 
 def weights(speeds, step, half, lane):
@@ -310,11 +328,20 @@
     for field in range(4):
         for x in range(4):
             for half in halves:
-                for at, edge_ref, corner_ref in ((1, low_x_ref, low_c_ref), (21, high_x_ref, high_c_ref)):
+                for at, edge_ref in ((1, low_x_ref), (21, high_x_ref)):
                     stage_ref[field, x + at, half, 8:40, :] = edge_ref[field * 4 + x, half]
-                    corner = corner_ref[field, x, half]
-                    stage_ref[field, x + at, half, 4:8, :] = corner[4:8]
-                    stage_ref[field, x + at, half, 40:44, :] = corner[0:4]
+    for at, (field, planes) in enumerate(corner_tiles):
+        for half in halves:
+            for corner_ref, low in ((low_c_ref, True), (high_c_ref, False)):
+                corner = corner_ref[at, half]
+                for place, far in enumerate(planes):
+                    x = 5 - far if low else 20 + far
+                    if len(planes) == 1:
+                        stage_ref[field, x, half, 4:8, :] = corner[4:8]
+                        stage_ref[field, x, half, 40:44, :] = corner[0:4]
+                    else:
+                        stage_ref[field, x, half, 6:8, :] = corner[4 * place + 2 : 4 * place + 4]
+                        stage_ref[field, x, half, 40:42, :] = corner[4 * place : 4 * place + 2]
     for half in halves:
         stage_ref[0, 0, half, 8:40, :] = low_x_ref[16, half]
     for pair in (0, 1, 6, 7):
@@ -351,7 +378,7 @@
         for half in halves:
             total_ref[half, rows_of_tile(tile), :] = ends_ref[1, half, tile]
     lines = [div_ref[:, half, 8:40, :].reshape(block_x * block_y, 128) for half in halves]
-    freq_ref[...] = dot(jnp.concatenate(lines, axis=1), table_ref[...], ((1,), (0,)))
+    freq_ref[...] = dot(data_side(jnp.concatenate(lines, axis=1), 1, 2), table_ref[...], ((1,), (0,)))
 
     def pack(step):
         for x in range(4):
@@ -424,19 +451,37 @@
         up_x_ref[16, half] = fifth[:, half * 128 : half * 128 + 128]
 
 
+corner_tiles = (
+    (0, (1,)), (0, (2, 3)), (1, (1,)), (1, (2,)), (1, (3, 4)), (2, (1, 2)), (3, (1, 2)),
+)
+
+
 def corner_kernel(low_y_ref, high_y_ref, up_ref, down_ref):
     row = lax.broadcasted_iota(jnp.int32, (8, 128), 0)
-    for field in range(4):
-        for x in range(4):
-            for half in range(2):
-                for at, ref in ((block_x - 4, up_ref), (0, down_ref)):
-                    high = high_y_ref[field, (at + x) // 2, half]
-                    low = low_y_ref[field, (at + x) // 2, half]
-                    if x % 2 == 0:
-                        low = pltpu.roll(low, 4, 0)
-                    else:
-                        high = pltpu.roll(high, 4, 0)
-                    ref[field, x, half] = jnp.where(row < 4, high, low)
+
+    def rows_at(field, x, half):
+        low, high = low_y_ref[field, x // 2, half], high_y_ref[field, x // 2, half]
+        if x % 2 == 0:
+            low = pltpu.roll(low, 4, 0)
+        else:
+            high = pltpu.roll(high, 4, 0)
+        return jnp.where(row < 4, high, low)
+
+    for at, (field, planes) in enumerate(corner_tiles):
+        for half in halves:
+            for ref, upward in ((up_ref, True), (down_ref, False)):
+                found = [
+                    rows_at(field, block_x - far if upward else far - 1, half) for far in planes
+                ]
+                if len(found) == 1:
+                    ref[at, half] = found[0]
+                else:
+                    near, far = found
+                    ref[at, half] = jnp.where(
+                        row < 4,
+                        jnp.where(row < 2, near, pltpu.roll(near, 4, 0)),
+                        jnp.where(row < 6, pltpu.roll(far, 4, 0), far),
+                    )
 
 
 def power_of(base, exponent, bits):
@@ -473,7 +518,7 @@
 ):
     place_x, place_y = lax.axis_index("gx"), lax.axis_index("gy")
     lines = [got_ref[:, part * 16 : part * 16 + 16, :].reshape(full_x, 128) for part in range(4)]
-    line_ref[...] = dot(jnp.concatenate(lines, axis=1), table_ref[...], ((0,), (0,)))
+    line_ref[...] = dot(data_side(jnp.concatenate(lines, axis=1), 0, 2), table_ref[...], ((0,), (0,)))
     lam = eigen_sum(eigen_ref, eigen_x_ref, place_x)
     rho, _ = roots_of(lam)
     special = lam == 0.0
@@ -551,7 +596,7 @@
         line_ref[rows, :] = jnp.where(special, level, scale * (here + enter_low))
         level = level + (here + flux_in - mean * (y + 1.0))
     line_ref[(block_y + 1) * 16 :, :] = jnp.zeros((112, full_x), jnp.float32)
-    found = dot(table_ref[...], line_ref[...], ((1,), (1,)))
+    found = dot(table_ref[...], data_side(line_ref[...], 1, 3), ((1,), (1,)))
     for part in range(5):
         lanes = slice(part * 128, part * 128 + 128)
         out_ref[:, part * 16 : part * 16 + 16, :] = found[:, lanes].reshape(count_x, block_x, 128)
@@ -596,10 +641,10 @@
     def shine(ref, shift, x, running):
         smoke = whole(ref, x - shift)
         depth = attenuation * smoke
-        series = 1.0 - depth * (1.0 / 7.0)
-        for order in (6.0, 5.0, 4.0, 3.0, 2.0):
+        series = 1.0 - depth * (1.0 / 5.0)
+        for order in (4.0, 3.0, 2.0):
             series = 1.0 - depth * (1.0 / order) * series
-        lost = jnp.where(jnp.abs(depth) < 0.25, depth * series, 1.0 - jnp.exp(-depth))
+        lost = jnp.where(jnp.abs(depth) < 0.0625, depth * series, 1.0 - jnp.exp(-depth))
         glow_ref[x] = jnp.exp(-attenuation * running) * lost * (1.0 / attenuation)
         glow_copy(x).start()
         return running + smoke
@@ -626,7 +671,7 @@
             )
     freq_ref[block_x, 32:40, :] = jnp.zeros((8, size_z), jnp.float32)
     press_ref[...] = dot(
-        freq_ref[...].reshape((block_x + 1) * 40, size_z), table_ref[...], ((1,), (0,))
+        data_side(freq_ref[...].reshape((block_x + 1) * 40, size_z), 1, 3), table_ref[...], ((1,), (0,))
     ).reshape(block_x + 1, 40, size_z)
     along_y = lax.broadcasted_iota(jnp.int32, (block_y, size_z), 0) + place_y * block_y
     along_z = lax.broadcasted_iota(jnp.int32, (block_y, size_z), 1)
@@ -765,12 +810,11 @@
         here,
     )(
         velocity, density, one, div_in, ends, low_x, high_x, low_y, high_y, low_c, high_c,
-        jnp.asarray(np.ascontiguousarray(table_z.T[:, turned])),
+        table_side(table_z.T[:, turned], 0, 2),
     )
     got = lax.all_to_all(
         packed.reshape(count_x, send_rows, 128), "gx", split_axis=0, concat_axis=0, tiled=True
     )
-    table_xt = jnp.asarray(np.ascontiguousarray(table_x.T))
     local, ends, moments, before = call(
         forward_kernel,
         (
@@ -782,7 +826,7 @@
         [(block_y * chunk_z, full_x)],
         4,
         {0: pltpu.SMEM},
-    )(eigen_z, got, eigen_x, table_xt)
+    )(eigen_z, got, eigen_x, table_side(table_x.T, 0, 2))
     moments = lax.all_to_all(moments, "gy", split_axis=0, concat_axis=0, tiled=True)
     back = call(
         backward_kernel,
@@ -790,7 +834,7 @@
         [(5 * 128, full_x)],
         4,
         {0: pltpu.SMEM},
-    )(eigen_z, local, ends, moments, eigen_x, table_xt, before)
+    )(eigen_z, local, ends, moments, eigen_x, table_side(table_x.T, 1, 3), before)
     back = lax.all_to_all(back, "gx", split_axis=0, concat_axis=0, tiled=True)
     return call(
         final_kernel,
@@ -807,7 +851,7 @@
         outside=2,
     )(
         back.reshape(count_x * back_rows, 128), lifted, lifted_in, smoke, smoke_in,
-        jnp.asarray(table_z),
+        table_side(table_z, 0, 3),
     )
 
 
@@ -832,7 +876,7 @@
     high_x = moved(down_x, "gx", False)
     low_y = moved(up_y, "gy", True)
     high_y = moved(down_y, "gy", False)
-    corner = shaped(4, 4, 2, 8, 128)
+    corner = shaped(len(corner_tiles), 2, 8, 128)
     up_c, down_c = call(corner_kernel, (corner, corner), [], 2)(low_y, high_y)
     low_c = moved(up_c, "gx", True)
     high_c = moved(down_c, "gx", False)

time: 106 us -> 105 us (level)
  no operation moved by 1% of the time
where the time goes in v2:
time: 105 us
  blocking collectives  57.1 us (54%)
  Pallas kernels  23.6 us (22%)
  starting transfers between devices  17.5 us (17%)
  waiting for transfers between devices  6.07 us (6%)
    pallas_call x7, Pallas kernels, run(): pl.pallas_call(kernel, out_shape=outs, in_specs=specs, out_specs=jax.tree...  23.6 us
    all_to_all x1, blocking collectives, step(): lax.all_to_all(moments, 'gy', split_axis=0, concat_axis=0, tiled=True)  22.6 us
    all_to_all x1, blocking collectives, step(): lax.all_to_all(packed.reshape(count_x, send_rows, 128), 'gx', split_axis=...  18.1 us
    ppermute x6, starting transfers between devices, moved(): return lax.ppermute(part, axis, pairs)  17.5 us
    all_to_all x1, blocking collectives, step(): back = lax.all_to_all(back, 'gx', split_axis=0, concat_axis=0, tiled=True)  16.3 us
    ppermute x6, waiting for transfers between devices, moved(): return lax.ppermute(part, axis, pairs)  6.07 us
  transfers between devices with their start and end apart: 6, of which 1 were waited for; matrix products, arithmetic and copies ran while one was open for 0% of the time, Pallas kernels for 8%

profile of v2, /device:TPU:1, one launch (start us, length us, event | category | flops | bytes accessed | tf_op | source)
XLA Modules:
  0.0 105.1 jit_solution(15726818717439102187)
XLA Ops:
  0.6 1.3 %shard_map.95 = (f32[17,2,32,128]{3,2,1,0:T(8,128)S(1)}, f32[16,2,32,128]{3,2,1,0:T(8,128)S(1)}, f32[5,8,2,8,128]{4,3,2,1,0:T(8,128)S(1)}, f32[4,8,2,8,128]{4,3,2,1,0:T(8,128)S(1)}) custom-call(bf16[3,16,32,256]{3,2,1,0:T(8,128)(2,1)} %velocity_hbm.5, bf16[16,32,256]{2,1,0:T(8,128)(2,1)} %density_hbm.5), custom_call_target="tpu_custom_call" | custom-call | flops 1000000000 | bytes 1024 | tf_op jit(solution)/shard_map/pallas_call | solution.py:729
  2.0 4.1 %collective-permute-start.2 = (f32[17,2,32,128]{3,2,1,0:T(8,128)S(1)}, f32[17,2,32,128]{3,2,1,0:T(8,128)S(1)}, u32[]{:S(2)}, u32[]{:S(2)}) collective-permute-start(f32[17,2,32,128]{3,2,1,0:T(8,128)S(1)} %get-tuple-element.25), channel_id=1, source_target_pairs={{0,16},{16,32},{32,48},{48,64},{64,80},{80,96},{96,112},{112,128},... | collective-permute-start | bytes 1671176 | tf_op jit(solution)/shard_map/ppermute | solution.py:860
  6.0 1.3 %collective-permute-start.3 = (f32[16,2,32,128]{3,2,1,0:T(8,128)S(1)}, f32[16,2,32,128]{3,2,1,0:T(8,128)S(1)}, u32[]{:S(2)}, u32[]{:S(2)}) collective-permute-start(f32[16,2,32,128]{3,2,1,0:T(8,128)S(1)} %get-tuple-element.26), channel_id=1, source_target_pairs={{16,0},{32,16},{48,32},{64,48},{80,64},{96,80},{112,96},{128,112},... | collective-permute-start | bytes 1572872 | tf_op jit(solution)/shard_map/ppermute | solution.py:860
  7.3 4.4 %collective-permute-start = (f32[5,8,2,8,128]{4,3,2,1,0:T(8,128)S(1)}, f32[5,8,2,8,128]{4,3,2,1,0:T(8,128)S(1)}, u32[]{:S(2)}, u32[]{:S(2)}) collective-permute-start(f32[5,8,2,8,128]{4,3,2,1,0:T(8,128)S(1)} %get-tuple-element.20), channel_id=1, source_target_pairs={{0,1},{1,2},{2,3},{3,4},{4,5},{5,6},{6,7},{7,8},{8,9},{9,10},{10,1... | collective-permute-start | bytes 983048 | tf_op jit(solution)/shard_map/ppermute | solution.py:860
  11.7 0.0 copy-start.1
  11.7 0.0 copy-start.3
  11.7 2.1 %collective-permute-start.1 = (f32[4,8,2,8,128]{4,3,2,1,0:T(8,128)S(1)}, f32[4,8,2,8,128]{4,3,2,1,0:T(8,128)S(1)}, u32[]{:S(2)}, u32[]{:S(2)}) collective-permute-start(f32[4,8,2,8,128]{4,3,2,1,0:T(8,128)S(1)} %get-tuple-element.21), channel_id=1, source_target_pairs={{1,0},{2,1},{3,2},{4,3},{5,4},{6,5},{7,6},{8,7},{9,8},{10,9},{11,1... | collective-permute-start | bytes 786440 | tf_op jit(solution)/shard_map/ppermute | solution.py:860
  13.8 6.1 %collective-permute-done.1.high_y_ref = f32[4,8,2,8,128]{4,3,2,1,0:T(8,128)S(1)} collective-permute-done((f32[4,8,2,8,128]{4,3,2,1,0:T(8,128)S(1)}, f32[4,8,2,8,128]{4,3,2,1,0:T(8,128)S(1)}, u32[]{:S(2)}, u32[]{:S(2)}) %collective-permute-start.1) | collective-permute-done | bytes 262176 | tf_op jit(solution)/shard_map/ppermute | solution.py:860
  19.9 0.0 collective-permute-done.low_y_ref
  19.9 4.3 %collective-permute-start.4 = (f32[7,2,8,128]{3,2,1,0:T(8,128)S(1)}, f32[7,2,8,128]{3,2,1,0:T(8,128)S(1)}, u32[]{:S(2)}, u32[]{:S(2)}) collective-permute-start(f32[7,2,8,128]{3,2,1,0:T(8,128)S(1)} %get-tuple-element.27), channel_id=1, source_target_pairs={{0,16},{16,32},{32,48},{48,64},{64,80},{80,96},{96,112},{112,128},... | collective-permute-start | bytes 172040 | tf_op jit(solution)/shard_map/ppermute | solution.py:860
  24.2 0.0 copy-start.2
  24.2 1.4 %collective-permute-start.5 = (f32[7,2,8,128]{3,2,1,0:T(8,128)S(1)}, f32[7,2,8,128]{3,2,1,0:T(8,128)S(1)}, u32[]{:S(2)}, u32[]{:S(2)}) collective-permute-start(f32[7,2,8,128]{3,2,1,0:T(8,128)S(1)} %get-tuple-element.28), channel_id=1, source_target_pairs={{16,0},{32,16},{48,32},{64,48},{80,64},{96,80},{112,96},{128,112},... | collective-permute-start | bytes 172040 | tf_op jit(solution)/shard_map/ppermute | solution.py:860
  25.6 0.0 copy-done.1
  25.6 0.0 copy-done.3
  25.6 8.5 %shard_map.96 = (f32[4,8,2,9,8,128]{5,4,3,2,1,0:T(8,128)S(1)}, f32[3,8,2,48,128]{4,3,2,1,0:T(8,128)S(1)}, f32[8,2,48,128]{3,2,1,0:T(8,128)S(1)}, f32[8,2,48,128]{3,2,1,0:T(8,128)S(1)}, f32[2,2,5,8,128]{4,3,2,1,0:T(8,128)S(1)}) custom-call(bf16[3,16,32,256]{3,2,1,0:T(8,128)(2,1)S(1)} %copy-done.1, bf16[16,32,256]{2,1,0:T(8,128)(2,1)S(1)} %copy-done.3, ...), custom_call_target="tpu_custom_call" | custom-call | flops 1000000000 | bytes 1024 | tf_op jit(solution)/shard_map/pallas_call | solution.py:729
  34.2 0.0 collective-permute-done.4.low_c_ref
  34.2 0.0 collective-permute-done.5.high_c_ref
  34.2 0.0 collective-permute-done.3.high_x_ref
  34.2 0.0 collective-permute-done.2.low_x_ref
  34.2 0.0 copy-done.2
  34.2 0.0 copy-start.4
  34.2 0.0 copy-start.6
  34.2 7.4 %shard_map.98 = (f32[3,8,2,48,128]{4,3,2,1,0:T(8,128)S(1)}, f32[8,2,48,128]{3,2,1,0:T(8,128)S(1)}, f32[1152,128]{1,0:T(8,128)S(1)}) custom-call(bf16[3,16,32,256]{3,2,1,0:T(8,128)(2,1)S(1)} %copy-done.1, bf16[16,32,256]{2,1,0:T(8,128)(2,1)S(1)} %copy-done.3, f32[4,8,2,9,8,128]{5,4,3,2,1,0:T(8,128)S(1)} %get-tuple-element.22.one_hbm, ...), custom_call_target="tpu_custom_call" | custom-call | flops 1000000000 | bytes 1024 | tf_op jit(solution)/shard_map/pallas_call | solution.py:729
  41.7 18.1 %all_to_all.15.got_ref = f32[16,72,128]{2,1,0:T(8,128)S(1)} all-to-all(f32[16,72,128]{2,1,0:T(8,128)S(1)} %bitcast.3), channel_id=1, replica_groups=mesh['gx'=16,'gy'=16] {'gx'}, dimensions={0} | all-to-all | bytes 1179648 | tf_op jit(solution)/shard_map/all_to_all | solution.py:815
  59.8 0.0 copy-done.4
  59.9 0.0 copy-done.6
  59.9 0.0 copy-start.5
  59.9 1.1 %shard_map.99 = (f32[512,256]{1,0:T(8,128)S(1)}, f32[2,16,256]{2,1,0:T(8,128)S(1)}, f32[16,16,256]{2,1,0:T(8,128)S(1)}, f32[16,8,128]{2,1,0:T(8,128)S(1)}) custom-call(f32[256]{0:T(256)S(1)} %copy-done.4, f32[16,72,128]{2,1,0:T(8,128)S(1)} %all_to_all.15.got_ref, f32[16,256]{1,0:T(8,128)S(1)} %jit_solution_.3.eigen_x_ref, bf16[768,256]{1,0:T(8,128)(2,1)S(1)} %copy-done.6), custom_call_target="tpu_custom_call" | custom-call | flops 1000000000 | bytes 1024 | tf_op jit(solution)/shard_map/pallas_call | solution.py:729
  60.9 22.6 %all_to_all.16.got_ref = f32[16,16,256]{2,1,0:T(8,128)S(1)} all-to-all(f32[16,16,256]{2,1,0:T(8,128)S(1)} %get-tuple-element.32), channel_id=1, replica_groups=mesh['gx'=16,'gy'=16] {'gy'}, dimensions={0} | all-to-all | bytes 524288 | tf_op jit(solution)/shard_map/all_to_all | solution.py:830
  83.6 0.0 copy-done.5
  83.6 1.6 %shard_map.100 = f32[16,88,128]{2,1,0:T(8,128)S(1)} custom-call(f32[256]{0:T(256)S(1)} %copy-done.4, f32[512,256]{1,0:T(8,128)S(1)} %get-tuple-element.30.local_ref, f32[2,16,256]{2,1,0:T(8,128)S(1)} %get-tuple-element.31.ends_ref, f32[16,16,256]{2,1,0:T(8,128)S(1)} %all_to_all.16.got_ref, f32[16,256]{1,0:T(8,128)S(1)} %jit_solution_.3.eigen_x_ref, ...), custom_call_target="tpu_custom_call" | custom-call | flops 1000000000 | bytes 1024 | tf_op jit(solution)/shard_map/pallas_call | solution.py:729
  85.2 0.0 copy-start
  85.2 16.3 %all_to_all.17 = f32[16,88,128]{2,1,0:T(8,128)S(1)} all-to-all(f32[16,88,128]{2,1,0:T(8,128)S(1)} %shard_map.100), channel_id=1, replica_groups=mesh['gx'=16,'gy'=16] {'gx'}, dimensions={0} | all-to-all | bytes 1441792 | tf_op jit(solution)/shard_map/all_to_all | solution.py:838
  101.5 0.0 copy-done
  101.5 3.6 %shard_map.101 = (f32[3,16,32,256]{3,2,1,0:T(8,128)}, f32[16,32,256]{2,1,0:T(8,128)}) custom-call(f32[1408,128]{1,0:T(8,128)S(1)} %bitcast.2, f32[3,8,2,48,128]{4,3,2,1,0:T(8,128)S(1)} %get-tuple-element.34.lifted_ref, f32[3,8,2,48,128]{4,3,2,1,0:T(8,128)S(1)} %get-tuple-element.35.lifted_in_ref, f32[8,2,48,128]{3,2,1,0:T(8,128)S(1)} %get-tuple-element.36.smoke_ref, ...), custom_call_target="tpu_custom_call" | custom-call | flops 1000000000 | bytes 1024 | tf_op jit(solution)/shard_map/pallas_call | solution.py:729
  (2 shorter events, 0.0 us)
Async XLA Ops:
  2.0 32.2 %collective-permute-start.2 = (f32[17,2,32,128]{3,2,1,0:T(8,128)S(1)}, f32[17,2,32,128]{3,2,1,0:T(8,128)S(1)}, u32[]{:S(2)}, u32[]{:S(2)}) collective-permute-start(f32[17,2,32,128]{3,2,1,0:T(8,128)S(1)} %get-tuple-element.25), channel_id=1, source_target_pairs={{0,16},{16,32},{32,48},{48,64},{64,80},{80,96},{96,112},{112,128},... | collective-permute-start | bytes 1671176 | tf_op jit(solution)/shard_map/ppermute | solution.py:860
  6.0 28.2 %collective-permute-start.3 = (f32[16,2,32,128]{3,2,1,0:T(8,128)S(1)}, f32[16,2,32,128]{3,2,1,0:T(8,128)S(1)}, u32[]{:S(2)}, u32[]{:S(2)}) collective-permute-start(f32[16,2,32,128]{3,2,1,0:T(8,128)S(1)} %get-tuple-element.26), channel_id=1, source_target_pairs={{16,0},{32,16},{48,32},{64,48},{80,64},{96,80},{112,96},{128,112},... | collective-permute-start | bytes 1572872 | tf_op jit(solution)/shard_map/ppermute | solution.py:860
  7.3 12.5 %collective-permute-start = (f32[5,8,2,8,128]{4,3,2,1,0:T(8,128)S(1)}, f32[5,8,2,8,128]{4,3,2,1,0:T(8,128)S(1)}, u32[]{:S(2)}, u32[]{:S(2)}) collective-permute-start(f32[5,8,2,8,128]{4,3,2,1,0:T(8,128)S(1)} %get-tuple-element.20), channel_id=1, source_target_pairs={{0,1},{1,2},{2,3},{3,4},{4,5},{5,6},{6,7},{7,8},{8,9},{9,10},{10,1... | collective-permute-start | bytes 983048 | tf_op jit(solution)/shard_map/ppermute | solution.py:860
  11.7 13.9 %copy-start.1 = (bf16[3,16,32,256]{3,2,1,0:T(8,128)(2,1)S(1)}, bf16[3,16,32,256]{3,2,1,0:T(8,128)(2,1)}, u32[]{:S(2)}) copy-start(bf16[3,16,32,256]{3,2,1,0:T(8,128)(2,1)} %velocity_hbm.5) | copy-start | bytes 2359300
  11.7 13.9 %copy-start.3 = (bf16[16,32,256]{2,1,0:T(8,128)(2,1)S(1)}, bf16[16,32,256]{2,1,0:T(8,128)(2,1)}, u32[]{:S(2)}) copy-start(bf16[16,32,256]{2,1,0:T(8,128)(2,1)} %density_hbm.5) | copy-start | bytes 786436
  11.7 8.1 %collective-permute-start.1 = (f32[4,8,2,8,128]{4,3,2,1,0:T(8,128)S(1)}, f32[4,8,2,8,128]{4,3,2,1,0:T(8,128)S(1)}, u32[]{:S(2)}, u32[]{:S(2)}) collective-permute-start(f32[4,8,2,8,128]{4,3,2,1,0:T(8,128)S(1)} %get-tuple-element.21), channel_id=1, source_target_pairs={{1,0},{2,1},{3,2},{4,3},{5,4},{6,5},{7,6},{8,7},{9,8},{10,9},{11,1... | collective-permute-start | bytes 786440 | tf_op jit(solution)/shard_map/ppermute | solution.py:860
  19.9 14.3 %collective-permute-start.4 = (f32[7,2,8,128]{3,2,1,0:T(8,128)S(1)}, f32[7,2,8,128]{3,2,1,0:T(8,128)S(1)}, u32[]{:S(2)}, u32[]{:S(2)}) collective-permute-start(f32[7,2,8,128]{3,2,1,0:T(8,128)S(1)} %get-tuple-element.27), channel_id=1, source_target_pairs={{0,16},{16,32},{32,48},{48,64},{64,80},{80,96},{96,112},{112,128},... | collective-permute-start | bytes 172040 | tf_op jit(solution)/shard_map/ppermute | solution.py:860
  24.2 10.0 %copy-start.2 = (bf16[768,256]{1,0:T(8,128)(2,1)S(1)}, bf16[768,256]{1,0:T(8,128)(2,1)}, u32[]{:S(2)}) copy-start(bf16[768,256]{1,0:T(8,128)(2,1)} %constant.12.clone.table_ref) | copy-start | bytes 1179652
  24.2 10.0 %collective-permute-start.5 = (f32[7,2,8,128]{3,2,1,0:T(8,128)S(1)}, f32[7,2,8,128]{3,2,1,0:T(8,128)S(1)}, u32[]{:S(2)}, u32[]{:S(2)}) collective-permute-start(f32[7,2,8,128]{3,2,1,0:T(8,128)S(1)} %get-tuple-element.28), channel_id=1, source_target_pairs={{16,0},{32,16},{48,32},{64,48},{80,64},{96,80},{112,96},{128,112},... | collective-permute-start | bytes 172040 | tf_op jit(solution)/shard_map/ppermute | solution.py:860
  34.2 25.6 %copy-start.4 = (f32[256]{0:T(256)S(1)}, f32[256]{0:T(256)}, u32[]{:S(2)}) copy-start(f32[256]{0:T(256)} %constant.10.clone.eigen_ref) | copy-start | bytes 3076
  34.2 25.6 %copy-start.6 = (bf16[768,256]{1,0:T(8,128)(2,1)S(1)}, bf16[768,256]{1,0:T(8,128)(2,1)}, u32[]{:S(2)}) copy-start(bf16[768,256]{1,0:T(8,128)(2,1)} %constant.13.clone.table_ref) | copy-start | bytes 1179652
  59.9 23.7 %copy-start.5 = (bf16[256,1536]{1,0:T(8,128)(2,1)S(1)}, bf16[256,1536]{1,0:T(8,128)(2,1)}, u32[]{:S(2)}) copy-start(bf16[256,1536]{1,0:T(8,128)(2,1)} %constant.14.clone.table_ref) | copy-start | bytes 2359300
  85.2 16.4 %copy-start = (bf16[1536,256]{1,0:T(8,128)(2,1)S(1)}, bf16[1536,256]{1,0:T(8,128)(2,1)}, u32[]{:S(2)}) copy-start(bf16[1536,256]{1,0:T(8,128)(2,1)} %constant.15.clone.table_ref) | copy-start | bytes 2359300

commit v3 on v2

--- a/solution.py
+++ b/solution.py
@@ -1,5 +1,3 @@
-import functools
-
 import jax
 import jax.numpy as jnp
 import numpy as np
@@ -274,7 +272,12 @@
     each(0, block_x, lambda x: fill_plane(stage_ref, x, velocity_ref, density_ref, x))
     each(0, block_x, lambda x: spread(stage_ref, raw_ref, x))
     section_one, _, plane = stencil(raw_ref, 0, one_ref, 2)
-    each(2, 14, section_one)
+
+    def both(step):
+        section_one(2 * step + 2)
+        section_one(2 * step + 3)
+
+    each(0, 6, both)
     one_copies = [
         pltpu.make_async_copy(
             one_ref.at[:, 8 * part : 8 * part + 4], one_hbm.at[:, 4 * part : 4 * part + 4], one_sent.at[part]
@@ -360,7 +363,13 @@
 
     each(0, 17, lambda at: spread(stage_ref, raw_ref, jnp.where(at < 9, at, at + 8)))
     section_one(-3, (0,))
-    each(0, 8, lambda at: section_one(jnp.where(at < 4, at - 2, at + 10)))
+
+    def both(step):
+        x = jnp.where(step < 2, 2 * step - 2, 2 * step + 10)
+        section_one(x)
+        section_one(x + 1)
+
+    each(0, 4, both)
     for copy in inner_copies:
         copy.wait()
     for tile in range(tiles):
@@ -652,7 +661,8 @@
     parts = ((0, 4, 0, lifted_ref, smoke_ref), (4, 12, 4, lifted_in_ref, smoke_in_ref),
              (12, 16, 8, lifted_ref, smoke_ref))
     for first, last, shift, _, ref in parts:
-        entered = lax.fori_loop(first, last, functools.partial(shine, ref, shift), entered)
+        for x in range(first, last):
+            entered = shine(ref, shift, x, entered)
 
     def unpack(step):
         for x in range(4):

time: 105 us -> 105 us (level)
  no operation moved by 1% of the time
where the time goes in v3:
time: 105 us; the launch traced here: 104 us
  blocking collectives  57.1 us (54%)
  Pallas kernels  22.6 us (22%)
  starting transfers between devices  17.5 us (17%)
  waiting for transfers between devices  6.07 us (6%)
    all_to_all x1, blocking collectives, step(): lax.all_to_all(moments, 'gy', split_axis=0, concat_axis=0, tiled=True)  22.6 us
    pallas_call x7, Pallas kernels, run(): pl.pallas_call(kernel, out_shape=outs, in_specs=specs, out_specs=jax.tree...  22.6 us
    all_to_all x1, blocking collectives, step(): lax.all_to_all(packed.reshape(count_x, send_rows, 128), 'gx', split_axis=...  18.1 us
    ppermute x6, starting transfers between devices, moved(): return lax.ppermute(part, axis, pairs)  17.5 us
    all_to_all x1, blocking collectives, step(): back = lax.all_to_all(back, 'gx', split_axis=0, concat_axis=0, tiled=True)  16.3 us
    ppermute x6, waiting for transfers between devices, moved(): return lax.ppermute(part, axis, pairs)  6.07 us
  transfers between devices with their start and end apart: 6, of which 1 were waited for; matrix products, arithmetic and copies ran while one was open for 0% of the time, Pallas kernels for 8%

profile of v3, /device:TPU:1, one launch (start us, length us, event | category | flops | bytes accessed | tf_op | source)
XLA Modules:
  0.0 104.1 jit_solution(8026208747460067218)
XLA Ops:
  0.6 1.3 %shard_map.95 = (f32[17,2,32,128]{3,2,1,0:T(8,128)S(1)}, f32[16,2,32,128]{3,2,1,0:T(8,128)S(1)}, f32[5,8,2,8,128]{4,3,2,1,0:T(8,128)S(1)}, f32[4,8,2,8,128]{4,3,2,1,0:T(8,128)S(1)}) custom-call(bf16[3,16,32,256]{3,2,1,0:T(8,128)(2,1)} %velocity_hbm.5, bf16[16,32,256]{2,1,0:T(8,128)(2,1)} %density_hbm.5), custom_call_target="tpu_custom_call" | custom-call | flops 1000000000 | bytes 1024 | tf_op jit(solution)/shard_map/pallas_call | solution.py:739
  2.0 4.1 %collective-permute-start.2 = (f32[17,2,32,128]{3,2,1,0:T(8,128)S(1)}, f32[17,2,32,128]{3,2,1,0:T(8,128)S(1)}, u32[]{:S(2)}, u32[]{:S(2)}) collective-permute-start(f32[17,2,32,128]{3,2,1,0:T(8,128)S(1)} %get-tuple-element.25), channel_id=1, source_target_pairs={{0,16},{16,32},{32,48},{48,64},{64,80},{80,96},{96,112},{112,128},... | collective-permute-start | bytes 1671176 | tf_op jit(solution)/shard_map/ppermute | solution.py:870
  6.0 1.3 %collective-permute-start.3 = (f32[16,2,32,128]{3,2,1,0:T(8,128)S(1)}, f32[16,2,32,128]{3,2,1,0:T(8,128)S(1)}, u32[]{:S(2)}, u32[]{:S(2)}) collective-permute-start(f32[16,2,32,128]{3,2,1,0:T(8,128)S(1)} %get-tuple-element.26), channel_id=1, source_target_pairs={{16,0},{32,16},{48,32},{64,48},{80,64},{96,80},{112,96},{128,112},... | collective-permute-start | bytes 1572872 | tf_op jit(solution)/shard_map/ppermute | solution.py:870
  7.3 4.4 %collective-permute-start = (f32[5,8,2,8,128]{4,3,2,1,0:T(8,128)S(1)}, f32[5,8,2,8,128]{4,3,2,1,0:T(8,128)S(1)}, u32[]{:S(2)}, u32[]{:S(2)}) collective-permute-start(f32[5,8,2,8,128]{4,3,2,1,0:T(8,128)S(1)} %get-tuple-element.20), channel_id=1, source_target_pairs={{0,1},{1,2},{2,3},{3,4},{4,5},{5,6},{6,7},{7,8},{8,9},{9,10},{10,1... | collective-permute-start | bytes 983048 | tf_op jit(solution)/shard_map/ppermute | solution.py:870
  11.7 0.0 copy-start.1
  11.7 0.0 copy-start.3
  11.7 2.1 %collective-permute-start.1 = (f32[4,8,2,8,128]{4,3,2,1,0:T(8,128)S(1)}, f32[4,8,2,8,128]{4,3,2,1,0:T(8,128)S(1)}, u32[]{:S(2)}, u32[]{:S(2)}) collective-permute-start(f32[4,8,2,8,128]{4,3,2,1,0:T(8,128)S(1)} %get-tuple-element.21), channel_id=1, source_target_pairs={{1,0},{2,1},{3,2},{4,3},{5,4},{6,5},{7,6},{8,7},{9,8},{10,9},{11,1... | collective-permute-start | bytes 786440 | tf_op jit(solution)/shard_map/ppermute | solution.py:870
  13.8 6.1 %collective-permute-done.1.high_y_ref = f32[4,8,2,8,128]{4,3,2,1,0:T(8,128)S(1)} collective-permute-done((f32[4,8,2,8,128]{4,3,2,1,0:T(8,128)S(1)}, f32[4,8,2,8,128]{4,3,2,1,0:T(8,128)S(1)}, u32[]{:S(2)}, u32[]{:S(2)}) %collective-permute-start.1) | collective-permute-done | bytes 262176 | tf_op jit(solution)/shard_map/ppermute | solution.py:870
  19.9 0.0 collective-permute-done.low_y_ref
  19.9 4.3 %collective-permute-start.4 = (f32[7,2,8,128]{3,2,1,0:T(8,128)S(1)}, f32[7,2,8,128]{3,2,1,0:T(8,128)S(1)}, u32[]{:S(2)}, u32[]{:S(2)}) collective-permute-start(f32[7,2,8,128]{3,2,1,0:T(8,128)S(1)} %get-tuple-element.27), channel_id=1, source_target_pairs={{0,16},{16,32},{32,48},{48,64},{64,80},{80,96},{96,112},{112,128},... | collective-permute-start | bytes 172040 | tf_op jit(solution)/shard_map/ppermute | solution.py:870
  24.2 0.0 copy-start.2
  24.2 1.4 %collective-permute-start.5 = (f32[7,2,8,128]{3,2,1,0:T(8,128)S(1)}, f32[7,2,8,128]{3,2,1,0:T(8,128)S(1)}, u32[]{:S(2)}, u32[]{:S(2)}) collective-permute-start(f32[7,2,8,128]{3,2,1,0:T(8,128)S(1)} %get-tuple-element.28), channel_id=1, source_target_pairs={{16,0},{32,16},{48,32},{64,48},{80,64},{96,80},{112,96},{128,112},... | collective-permute-start | bytes 172040 | tf_op jit(solution)/shard_map/ppermute | solution.py:870
  25.6 0.0 copy-done.1
  25.6 0.0 copy-done.3
  25.6 8.0 %shard_map.96 = (f32[4,8,2,9,8,128]{5,4,3,2,1,0:T(8,128)S(1)}, f32[3,8,2,48,128]{4,3,2,1,0:T(8,128)S(1)}, f32[8,2,48,128]{3,2,1,0:T(8,128)S(1)}, f32[8,2,48,128]{3,2,1,0:T(8,128)S(1)}, f32[2,2,5,8,128]{4,3,2,1,0:T(8,128)S(1)}) custom-call(bf16[3,16,32,256]{3,2,1,0:T(8,128)(2,1)S(1)} %copy-done.1, bf16[16,32,256]{2,1,0:T(8,128)(2,1)S(1)} %copy-done.3, ...), custom_call_target="tpu_custom_call" | custom-call | flops 1000000000 | bytes 1024 | tf_op jit(solution)/shard_map/pallas_call | solution.py:739
  33.7 0.0 collective-permute-done.4.low_c_ref
  33.7 0.0 collective-permute-done.5.high_c_ref
  33.7 0.0 collective-permute-done.3.high_x_ref
  33.7 0.0 collective-permute-done.2.low_x_ref
  33.7 0.0 copy-done.2
  33.7 0.0 copy-start.4
  33.7 0.0 copy-start.6
  33.8 7.1 %shard_map.98 = (f32[3,8,2,48,128]{4,3,2,1,0:T(8,128)S(1)}, f32[8,2,48,128]{3,2,1,0:T(8,128)S(1)}, f32[1152,128]{1,0:T(8,128)S(1)}) custom-call(bf16[3,16,32,256]{3,2,1,0:T(8,128)(2,1)S(1)} %copy-done.1, bf16[16,32,256]{2,1,0:T(8,128)(2,1)S(1)} %copy-done.3, f32[4,8,2,9,8,128]{5,4,3,2,1,0:T(8,128)S(1)} %get-tuple-element.22.one_hbm, ...), custom_call_target="tpu_custom_call" | custom-call | flops 1000000000 | bytes 1024 | tf_op jit(solution)/shard_map/pallas_call | solution.py:739
  40.9 18.1 %all_to_all.15.got_ref = f32[16,72,128]{2,1,0:T(8,128)S(1)} all-to-all(f32[16,72,128]{2,1,0:T(8,128)S(1)} %bitcast.3), channel_id=1, replica_groups=mesh['gx'=16,'gy'=16] {'gx'}, dimensions={0} | all-to-all | bytes 1179648 | tf_op jit(solution)/shard_map/all_to_all | solution.py:825
  59.0 0.0 copy-done.4
  59.0 0.0 copy-done.6
  59.0 0.0 copy-start.5
  59.1 1.1 %shard_map.99 = (f32[512,256]{1,0:T(8,128)S(1)}, f32[2,16,256]{2,1,0:T(8,128)S(1)}, f32[16,16,256]{2,1,0:T(8,128)S(1)}, f32[16,8,128]{2,1,0:T(8,128)S(1)}) custom-call(f32[256]{0:T(256)S(1)} %copy-done.4, f32[16,72,128]{2,1,0:T(8,128)S(1)} %all_to_all.15.got_ref, f32[16,256]{1,0:T(8,128)S(1)} %jit_solution_.3.eigen_x_ref, bf16[768,256]{1,0:T(8,128)(2,1)S(1)} %copy-done.6), custom_call_target="tpu_custom_call" | custom-call | flops 1000000000 | bytes 1024 | tf_op jit(solution)/shard_map/pallas_call | solution.py:739
  60.1 22.6 %all_to_all.16.got_ref = f32[16,16,256]{2,1,0:T(8,128)S(1)} all-to-all(f32[16,16,256]{2,1,0:T(8,128)S(1)} %get-tuple-element.32), channel_id=1, replica_groups=mesh['gx'=16,'gy'=16] {'gy'}, dimensions={0} | all-to-all | bytes 524288 | tf_op jit(solution)/shard_map/all_to_all | solution.py:840
  82.8 0.0 copy-done.5
  82.8 1.6 %shard_map.100 = f32[16,88,128]{2,1,0:T(8,128)S(1)} custom-call(f32[256]{0:T(256)S(1)} %copy-done.4, f32[512,256]{1,0:T(8,128)S(1)} %get-tuple-element.30.local_ref, f32[2,16,256]{2,1,0:T(8,128)S(1)} %get-tuple-element.31.ends_ref, f32[16,16,256]{2,1,0:T(8,128)S(1)} %all_to_all.16.got_ref, f32[16,256]{1,0:T(8,128)S(1)} %jit_solution_.3.eigen_x_ref, ...), custom_call_target="tpu_custom_call" | custom-call | flops 1000000000 | bytes 1024 | tf_op jit(solution)/shard_map/pallas_call | solution.py:739
  84.4 0.0 copy-start
  84.4 16.3 %all_to_all.17 = f32[16,88,128]{2,1,0:T(8,128)S(1)} all-to-all(f32[16,88,128]{2,1,0:T(8,128)S(1)} %shard_map.100), channel_id=1, replica_groups=mesh['gx'=16,'gy'=16] {'gx'}, dimensions={0} | all-to-all | bytes 1441792 | tf_op jit(solution)/shard_map/all_to_all | solution.py:848
  100.7 0.0 copy-done
  100.7 3.4 %shard_map.101 = (f32[3,16,32,256]{3,2,1,0:T(8,128)}, f32[16,32,256]{2,1,0:T(8,128)}) custom-call(f32[1408,128]{1,0:T(8,128)S(1)} %bitcast.2, f32[3,8,2,48,128]{4,3,2,1,0:T(8,128)S(1)} %get-tuple-element.34.lifted_ref, f32[3,8,2,48,128]{4,3,2,1,0:T(8,128)S(1)} %get-tuple-element.35.lifted_in_ref, f32[8,2,48,128]{3,2,1,0:T(8,128)S(1)} %get-tuple-element.36.smoke_ref, ...), custom_call_target="tpu_custom_call" | custom-call | flops 1000000000 | bytes 1024 | tf_op jit(solution)/shard_map/pallas_call | solution.py:739
  (2 shorter events, 0.0 us)
Async XLA Ops:
  2.0 31.8 %collective-permute-start.2 = (f32[17,2,32,128]{3,2,1,0:T(8,128)S(1)}, f32[17,2,32,128]{3,2,1,0:T(8,128)S(1)}, u32[]{:S(2)}, u32[]{:S(2)}) collective-permute-start(f32[17,2,32,128]{3,2,1,0:T(8,128)S(1)} %get-tuple-element.25), channel_id=1, source_target_pairs={{0,16},{16,32},{32,48},{48,64},{64,80},{80,96},{96,112},{112,128},... | collective-permute-start | bytes 1671176 | tf_op jit(solution)/shard_map/ppermute | solution.py:870
  6.0 27.7 %collective-permute-start.3 = (f32[16,2,32,128]{3,2,1,0:T(8,128)S(1)}, f32[16,2,32,128]{3,2,1,0:T(8,128)S(1)}, u32[]{:S(2)}, u32[]{:S(2)}) collective-permute-start(f32[16,2,32,128]{3,2,1,0:T(8,128)S(1)} %get-tuple-element.26), channel_id=1, source_target_pairs={{16,0},{32,16},{48,32},{64,48},{80,64},{96,80},{112,96},{128,112},... | collective-permute-start | bytes 1572872 | tf_op jit(solution)/shard_map/ppermute | solution.py:870
  7.3 12.5 %collective-permute-start = (f32[5,8,2,8,128]{4,3,2,1,0:T(8,128)S(1)}, f32[5,8,2,8,128]{4,3,2,1,0:T(8,128)S(1)}, u32[]{:S(2)}, u32[]{:S(2)}) collective-permute-start(f32[5,8,2,8,128]{4,3,2,1,0:T(8,128)S(1)} %get-tuple-element.20), channel_id=1, source_target_pairs={{0,1},{1,2},{2,3},{3,4},{4,5},{5,6},{6,7},{7,8},{8,9},{9,10},{10,1... | collective-permute-start | bytes 983048 | tf_op jit(solution)/shard_map/ppermute | solution.py:870
  11.7 13.9 %copy-start.1 = (bf16[3,16,32,256]{3,2,1,0:T(8,128)(2,1)S(1)}, bf16[3,16,32,256]{3,2,1,0:T(8,128)(2,1)}, u32[]{:S(2)}) copy-start(bf16[3,16,32,256]{3,2,1,0:T(8,128)(2,1)} %velocity_hbm.5) | copy-start | bytes 2359300
  11.7 13.9 %copy-start.3 = (bf16[16,32,256]{2,1,0:T(8,128)(2,1)S(1)}, bf16[16,32,256]{2,1,0:T(8,128)(2,1)}, u32[]{:S(2)}) copy-start(bf16[16,32,256]{2,1,0:T(8,128)(2,1)} %density_hbm.5) | copy-start | bytes 786436
  11.7 8.1 %collective-permute-start.1 = (f32[4,8,2,8,128]{4,3,2,1,0:T(8,128)S(1)}, f32[4,8,2,8,128]{4,3,2,1,0:T(8,128)S(1)}, u32[]{:S(2)}, u32[]{:S(2)}) collective-permute-start(f32[4,8,2,8,128]{4,3,2,1,0:T(8,128)S(1)} %get-tuple-element.21), channel_id=1, source_target_pairs={{1,0},{2,1},{3,2},{4,3},{5,4},{6,5},{7,6},{8,7},{9,8},{10,9},{11,1... | collective-permute-start | bytes 786440 | tf_op jit(solution)/shard_map/ppermute | solution.py:870
  19.9 13.8 %collective-permute-start.4 = (f32[7,2,8,128]{3,2,1,0:T(8,128)S(1)}, f32[7,2,8,128]{3,2,1,0:T(8,128)S(1)}, u32[]{:S(2)}, u32[]{:S(2)}) collective-permute-start(f32[7,2,8,128]{3,2,1,0:T(8,128)S(1)} %get-tuple-element.27), channel_id=1, source_target_pairs={{0,16},{16,32},{32,48},{48,64},{64,80},{80,96},{96,112},{112,128},... | collective-permute-start | bytes 172040 | tf_op jit(solution)/shard_map/ppermute | solution.py:870
  24.2 9.6 %copy-start.2 = (bf16[768,256]{1,0:T(8,128)(2,1)S(1)}, bf16[768,256]{1,0:T(8,128)(2,1)}, u32[]{:S(2)}) copy-start(bf16[768,256]{1,0:T(8,128)(2,1)} %constant.12.clone.table_ref) | copy-start | bytes 1179652
  24.2 9.5 %collective-permute-start.5 = (f32[7,2,8,128]{3,2,1,0:T(8,128)S(1)}, f32[7,2,8,128]{3,2,1,0:T(8,128)S(1)}, u32[]{:S(2)}, u32[]{:S(2)}) collective-permute-start(f32[7,2,8,128]{3,2,1,0:T(8,128)S(1)} %get-tuple-element.28), channel_id=1, source_target_pairs={{16,0},{32,16},{48,32},{64,48},{80,64},{96,80},{112,96},{128,112},... | collective-permute-start | bytes 172040 | tf_op jit(solution)/shard_map/ppermute | solution.py:870
  33.7 25.3 %copy-start.4 = (f32[256]{0:T(256)S(1)}, f32[256]{0:T(256)}, u32[]{:S(2)}) copy-start(f32[256]{0:T(256)} %constant.10.clone.eigen_ref) | copy-start | bytes 3076
  33.7 25.3 %copy-start.6 = (bf16[768,256]{1,0:T(8,128)(2,1)S(1)}, bf16[768,256]{1,0:T(8,128)(2,1)}, u32[]{:S(2)}) copy-start(bf16[768,256]{1,0:T(8,128)(2,1)} %constant.13.clone.table_ref) | copy-start | bytes 1179652
  59.0 23.7 %copy-start.5 = (bf16[256,1536]{1,0:T(8,128)(2,1)S(1)}, bf16[256,1536]{1,0:T(8,128)(2,1)}, u32[]{:S(2)}) copy-start(bf16[256,1536]{1,0:T(8,128)(2,1)} %constant.14.clone.table_ref) | copy-start | bytes 2359300
  84.4 16.4 %copy-start = (bf16[1536,256]{1,0:T(8,128)(2,1)S(1)}, bf16[1536,256]{1,0:T(8,128)(2,1)}, u32[]{:S(2)}) copy-start(bf16[1536,256]{1,0:T(8,128)(2,1)} %constant.15.clone.table_ref) | copy-start | bytes 2359300
